TPU v7x, 256 devices: a whole 4x4x8 slice. The times are simulated.
256 devices in a mesh: col: 16 (over z, core), row: 16 (over x, y).
Axes of the slice: x: 4, y: 4, z: 8, core: 2. Of those that a mesh axis runs over, the one named last changes fastest.
Arguments:
- visibility: float32 [128, 2, 1024], P('row'), may hold values from -6 to 6
- baseline_uv: float32 [128, 2, 1024], P('row'), may hold values from 0 to 1024
- offsets: int32 [128, 2], P('row'), may hold values from 0 to 32767
- counts: int32 [128], P('row'), may hold values from 1 to 1024, 81920 in all
- taper_x: float32 [1024], replicated, may hold values from 0.1 to 1.9
- taper_y: float32 [1024], replicated, may hold values from 0.1 to 1.9
Outputs:
- image: float32 [2, 1024, 1024], P(None, 'col', 'row')
Inputs may be any that keep to these rules, and one draw needn't show every extreme that they name: subgrid s has live visibilities in its first counts[s] slots; the other slots hold data that must be ignored.
All inputs are finite; a program needn't handle non-finite values. No bound on the sum of `counts` on one device may be relied on, other than what follows from the above.
Results may differ from a plain program's by a relative error of at most 0.0063.
Values may be sent and summed in bfloat16 or wider, within the bound.
A program may use at most 128 MiB of HBM per device.

v0:
```python
import math

import jax
import jax.numpy as jnp
from jax import lax
from jax.sharding import PartitionSpec as P

IMAGE = 32768
VIS_BLOCK = 256


def sample_pixels(grid_side):
    position = jnp.arange(grid_side, dtype=jnp.int32)
    stride = IMAGE // grid_side - 1
    return jnp.mod(stride * position - IMAGE // 2, IMAGE)


def dft_tables(grid_side):
    position = jnp.arange(grid_side, dtype=jnp.int32)
    pixels = sample_pixels(grid_side)
    turn_count = jnp.mod(pixels[:, None] * position[None, :], IMAGE)
    angles = 2.0 * math.pi / IMAGE * turn_count.astype(jnp.float32)
    return (jnp.cos(angles).astype(jnp.bfloat16), jnp.sin(angles).astype(jnp.bfloat16))


def offset_phases(offset_col, grid_side):
    pixels = sample_pixels(grid_side)
    shifted = jnp.mod(offset_col, IMAGE)
    turn_count = jnp.mod(pixels[None, :] * shifted[:, None], IMAGE)
    angles = 2.0 * math.pi / IMAGE * turn_count.astype(jnp.float32)
    return (jnp.cos(angles), jnp.sin(angles))


def grid_slab(visibility, baseline_uv, counts, column_first, slab_width, grid_side):
    position = jnp.arange(grid_side, dtype=jnp.float32)
    slab_cols = column_first.astype(jnp.float32) + jnp.arange(slab_width, dtype=jnp.float32)
    chirp_rate = math.pi / grid_side

    def one_subgrid(inputs):
        vis_rows, uv_rows, live_count = inputs

        def add_block(block_index, running):
            first_row = block_index * VIS_BLOCK
            vis_part = lax.dynamic_slice_in_dim(vis_rows, first_row, VIS_BLOCK, 1)
            uv_part = lax.dynamic_slice_in_dim(uv_rows, first_row, VIS_BLOCK, 1)
            live_mask = (first_row + jnp.arange(VIS_BLOCK, dtype=jnp.int32) < live_count).astype(
                jnp.float32
            )
            kernel_u = jnp.cos(chirp_rate * (position[None, :] - uv_part[0][:, None]) ** 2).astype(
                jnp.bfloat16
            )
            kernel_v = jnp.cos(chirp_rate * (slab_cols[None, :] - uv_part[1][:, None]) ** 2)
            weighted = jnp.concatenate(
                [
                    (vis_part[0] * live_mask)[:, None] * kernel_v,
                    (vis_part[1] * live_mask)[:, None] * kernel_v,
                ],
                axis=1,
            ).astype(jnp.bfloat16)
            return running + lax.dot_general(
                kernel_u, weighted, (((0,), (0,)), ((), ())), preferred_element_type=jnp.float32
            )

        block_total = (live_count + VIS_BLOCK - 1) // VIS_BLOCK
        running = lax.fori_loop(
            0, block_total, add_block, jnp.zeros((grid_side, 2 * slab_width), jnp.float32)
        )
        return running.astype(jnp.bfloat16)

    return lax.map(one_subgrid, (visibility, baseline_uv, counts))


def combine_rows(product, grid_side):
    real_raw = product[:, 0, :, :grid_side] - product[:, 1, :, grid_side:]
    imag_raw = product[:, 0, :, grid_side:] + product[:, 1, :, :grid_side]
    return (real_raw, imag_raw)


def apply_phase(real_raw, imag_raw, cos_v, sin_v, taper_y, norm_scale):
    out_real = taper_y[None, None, :] * (
        cos_v[:, None, :] * real_raw - sin_v[:, None, :] * imag_raw
    )
    out_imag = taper_y[None, None, :] * (
        cos_v[:, None, :] * imag_raw + sin_v[:, None, :] * real_raw
    )
    return norm_scale * jnp.stack([jnp.sum(out_real, axis=0), jnp.sum(out_imag, axis=0)])


def per_device(visibility, baseline_uv, offsets, counts, taper_x, taper_y):
    grid_side = taper_x.shape[0]
    col_count = lax.axis_size("col")
    row_count = lax.axis_size("row")
    slab_width = grid_side // col_count
    facet_y = grid_side // row_count
    groups = visibility.shape[0]
    norm_scale = 4.0 / (grid_side * math.sqrt(groups * row_count * visibility.shape[2]))
    column_first = lax.axis_index("col") * slab_width
    table_re, table_im = dft_tables(grid_side)
    stacked = jnp.concatenate([table_re, table_im], axis=0)
    ucos, usin = offset_phases(offsets[:, 0], grid_side)
    vcos, vsin = offset_phases(offsets[:, 1], grid_side)
    subgrids = grid_slab(visibility, baseline_uv, counts, column_first, slab_width, grid_side)
    product = jnp.einsum("aj,sjk->sak", stacked, subgrids, preferred_element_type=jnp.float32)
    real_raw = product[:, :grid_side, :slab_width] - product[:, grid_side:, slab_width:]
    imag_raw = product[:, :grid_side, slab_width:] + product[:, grid_side:, :slab_width]
    col_real = taper_x[None, :, None] * (ucos[:, :, None] * real_raw - usin[:, :, None] * imag_raw)
    col_imag = taper_x[None, :, None] * (ucos[:, :, None] * imag_raw + usin[:, :, None] * real_raw)
    columns = jnp.stack([col_real, col_imag], axis=1).astype(jnp.bfloat16)
    product_rows = jnp.einsum(
        "scik,ak->scia",
        lax.all_to_all(columns, "col", split_axis=2, concat_axis=3, tiled=True),
        stacked,
        preferred_element_type=jnp.float32,
    )
    row_real, row_imag = combine_rows(product_rows, grid_side)
    rows_out = jnp.stack([row_real, row_imag], axis=1)
    partial_rows = apply_phase(rows_out[:, 0], rows_out[:, 1], vcos, vsin, taper_y, norm_scale)
    everything = lax.psum(partial_rows, "row")
    return lax.dynamic_slice_in_dim(everything, lax.axis_index("row") * facet_y, facet_y, 2)


def solution(mesh):
    placed = (P("row", None, None), P("row", None, None), P("row", None), P("row"), P(), P())
    return jax.shard_map(
        per_device, mesh=mesh, in_specs=placed, out_specs=P(None, "col", "row"), check_vma=False
    )
```

profile of v0, /device:TPU:1, one launch (start us, length us, event | category | flops | bytes accessed | tf_op | source)
XLA Modules:
  0.0 392.5 jit_solution(14350504417535493547)
XLA Ops:
  7.3 132.4 %while.49 = (s32[]{:T(128)}, bf16[8,1024,128]{2,1,0:T(8,128)(2,1)}, s32[8]{0:T(128)}, f32[8,2,1024]{2,1,0:T(2,128)}, f32[8,2,1024]{2,1,0:T(2,128)}, /*index=5*/f...) while((s32[]{:T(128)}, bf16[8,1024,128]{2,1,0:T(8,128)(2,1)}, ...), condition=%wide.region_3.4_spmd.clone, body=%wide.region_0.3_spmd.clone.sunk | while | flops 68666456 | bytes 2548898 | solution.py:70
  9.9 9.6 %while.50 = (s32[]{:T(128)}, f32[1024,128]{1,0:T(8,128)S(1)}, s32[]{:T(128)}, f32[1024]{0:T(1024)S(1)}, f32[2,1024]{1,0:T(2,128)S(1)}, /*index=5*/s32[]{:T(128)}...) while((s32[]{:T(128)}, f32[1024,128]{1,0:T(8,128)S(1)}, ...), condition=%wide.region_2.2_spmd, body=%wide.region_1.1_spmd.sunk | while | flops 68535304 | bytes 1200591 | solution.py:65
  15.8 3.8 convolution_add_fusion.2
  22.9 9.6 %while.50 = (s32[]{:T(128)}, f32[1024,128]{1,0:T(8,128)S(1)}, s32[]{:T(128)}, f32[1024]{0:T(1024)S(1)}, f32[2,1024]{1,0:T(2,128)S(1)}, /*index=5*/s32[]{:T(128)}...) while((s32[]{:T(128)}, f32[1024,128]{1,0:T(8,128)S(1)}, ...), condition=%wide.region_2.2_spmd, body=%wide.region_1.1_spmd.sunk | while | flops 68535304 | bytes 1200591 | solution.py:65
  28.7 3.8 convolution_add_fusion.2
  35.8 14.4 %while.50 = (s32[]{:T(128)}, f32[1024,128]{1,0:T(8,128)S(1)}, s32[]{:T(128)}, f32[1024]{0:T(1024)S(1)}, f32[2,1024]{1,0:T(2,128)S(1)}, /*index=5*/s32[]{:T(128)}...) while((s32[]{:T(128)}, f32[1024,128]{1,0:T(8,128)S(1)}, ...), condition=%wide.region_2.2_spmd, body=%wide.region_1.1_spmd.sunk | while | flops 68535304 | bytes 1200591 | solution.py:65
  41.7 3.8 convolution_add_fusion.2
  46.5 3.8 convolution_add_fusion.2
  53.5 14.4 %while.50 = (s32[]{:T(128)}, f32[1024,128]{1,0:T(8,128)S(1)}, s32[]{:T(128)}, f32[1024]{0:T(1024)S(1)}, f32[2,1024]{1,0:T(2,128)S(1)}, /*index=5*/s32[]{:T(128)}...) while((s32[]{:T(128)}, f32[1024,128]{1,0:T(8,128)S(1)}, ...), condition=%wide.region_2.2_spmd, body=%wide.region_1.1_spmd.sunk | while | flops 68535304 | bytes 1200591 | solution.py:65
  54.6 3.8 convolution_add_fusion.2
  64.2 3.8 convolution_add_fusion.2
  71.3 19.3 %while.50 = (s32[]{:T(128)}, f32[1024,128]{1,0:T(8,128)S(1)}, s32[]{:T(128)}, f32[1024]{0:T(1024)S(1)}, f32[2,1024]{1,0:T(2,128)S(1)}, /*index=5*/s32[]{:T(128)}...) while((s32[]{:T(128)}, f32[1024,128]{1,0:T(8,128)S(1)}, ...), condition=%wide.region_2.2_spmd, body=%wide.region_1.1_spmd.sunk | while | flops 68535304 | bytes 1200591 | solution.py:65
  72.3 3.8 convolution_add_fusion.2
  82.0 3.8 convolution_add_fusion.2
  86.8 3.8 convolution_add_fusion.2
  93.9 14.4 %while.50 = (s32[]{:T(128)}, f32[1024,128]{1,0:T(8,128)S(1)}, s32[]{:T(128)}, f32[1024]{0:T(1024)S(1)}, f32[2,1024]{1,0:T(2,128)S(1)}, /*index=5*/s32[]{:T(128)}...) while((s32[]{:T(128)}, f32[1024,128]{1,0:T(8,128)S(1)}, ...), condition=%wide.region_2.2_spmd, body=%wide.region_1.1_spmd.sunk | while | flops 68535304 | bytes 1200591 | solution.py:65
  99.7 3.8 convolution_add_fusion.2
  111.6 14.4 %while.50 = (s32[]{:T(128)}, f32[1024,128]{1,0:T(8,128)S(1)}, s32[]{:T(128)}, f32[1024]{0:T(1024)S(1)}, f32[2,1024]{1,0:T(2,128)S(1)}, /*index=5*/s32[]{:T(128)}...) while((s32[]{:T(128)}, f32[1024,128]{1,0:T(8,128)S(1)}, ...), condition=%wide.region_2.2_spmd, body=%wide.region_1.1_spmd.sunk | while | flops 68535304 | bytes 1200591 | solution.py:65
  117.5 3.8 convolution_add_fusion.2
  122.3 3.8 convolution_add_fusion.2
  129.4 9.6 %while.50 = (s32[]{:T(128)}, f32[1024,128]{1,0:T(8,128)S(1)}, s32[]{:T(128)}, f32[1024]{0:T(1024)S(1)}, f32[2,1024]{1,0:T(2,128)S(1)}, /*index=5*/s32[]{:T(128)}...) while((s32[]{:T(128)}, f32[1024,128]{1,0:T(8,128)S(1)}, ...), condition=%wide.region_2.2_spmd, body=%wide.region_1.1_spmd.sunk | while | flops 68535304 | bytes 1200591 | solution.py:65
  130.4 3.8 convolution_add_fusion.2
  139.8 18.0 %cosine_convert_fusion.2 = (bf16[1024,1024]{1,0:T(8,128)(2,1)S(1)}, bf16[1024,1024]{1,0:T(8,128)(2,1)S(1)}) fusion(s32[1024]{0:T(1024)S(1)} %add_select_fusion.3), kind=kLoop, calls=%fused_computation.37 | loop fusion | flops 16777216 | bytes 4198400 | tf_op jit(solution)/shard_map/convert_element_type | solution.py:23
  158.1 4.6 %convolution_bitcast_fusion = f32[8,2048,128]{1,2,0:T(8,128)S(1)} fusion(bf16[8,1024,128]{2,1,0:T(8,128)(2,1)S(1)} %copy-done.4, bf16[1024,1024]{1,0:T(8,128)(2,1)S(1)} %get-tuple-element.277, bf16[1024,1024]{1,0:T(8,128)(2,1)S(1)} %get-tuple-element.276), kind=kOutput, calls=%fused_computation.27 | convolution fusion | flops 4303355904 | bytes 14680064 | tf_op jit(solution)/shard_map/aj,sjk->sak/dot_general | solution.py:103
  164.2 5.1 %copy.17 = bf16[8,2,1024,64]{3,0,1,2:T(8,128)(2,1)} copy(bf16[8,2,1024,64]{2,3,0,1:T(8,128)(2,1)S(1)} %pad_maximum_fusion.3) | data formatting | bytes 4194304 | tf_op jit(solution)/shard_map/stack | solution.py:108
  169.2 6.3 %reshape.193 = bf16[16,2,32768]{2,1,0:T(2,128)(2,1)S(1)} reshape(bf16[1024,2,8,64]{3,2,1,0:T(8,128)(2,1)} %bitcast.85) | data formatting | bytes 4194304
  175.6 60.9 %all_to_all.18 = bf16[16,2,32768]{2,1,0:T(2,128)(2,1)} all-to-all(bf16[16,2,32768]{2,1,0:T(2,128)(2,1)S(1)} %reshape.193), channel_id=1, replica_groups=mesh['col'=16,'row'=16] {'col'}, dimensions={0} | all-to-all | bytes 4194304 | tf_op jit(solution)/shard_map/all_to_all | solution.py:111
  236.5 7.4 %reshape.194 = bf16[1024,2,8,64]{3,2,1,0:T(8,128)(2,1)} reshape(bf16[16,2,32768]{2,1,0:T(2,128)(2,1)} %all_to_all.18) | data formatting | bytes 4194304
  243.9 6.9 %copy.26 = bf16[8,2,16,64,64]{4,2,3,1,0:T(8,128)(2,1)} copy(bf16[8,2,16,64,64]{4,0,1,3,2:T(8,128)(2,1)} %bitcast.86) | data formatting | bytes 4194304 | tf_op jit(solution)/shard_map/all_to_all | solution.py:111
  250.7 5.5 %all_to_all.16 = bf16[8,2,64,1024]{3,2,1,0:T(8,128)(2,1)S(1)} reshape(bf16[8,2,64,16,64]{4,3,2,1,0:T(8,128)(2,1)} %bitcast.87) | data formatting | bytes 4194304 | tf_op jit(solution)/shard_map/all_to_all | solution.py:111
  256.2 6.6 %fusion.17 = f32[8,2,64,2048]{3,2,1,0:T(8,128)S(1)} fusion(bf16[8,2,64,1024]{3,2,1,0:T(8,128)(2,1)S(1)} %all_to_all.16, bf16[1024,1024]{1,0:T(8,128)(2,1)} %copy-done.1, bf16[1024,1024]{1,0:T(8,128)(2,1)} %copy-done), kind=kOutput, calls=%fused_computation.32 | convolution fusion | flops 4303355904 | bytes 14680064 | tf_op jit(solution)/shard_map/scik,ak->scia/dot_general | solution.py:109
  264.8 119.3 %all-reduce.2.cloned.1.call-done = f32[2,64,1024]{2,1,0:T(8,128)} async-done(((f32[2,64,1024]{2,1,0:T(8,128)}), f32[2,64,1024]{2,1,0:T(8,128)}) %all-reduce.2.cloned.1.call-update) | async-done | bytes 524304 | tf_op jit(solution)/shard_map/psum | solution.py:118
  (166 shorter events, 83.9 us)
Async XLA Ops:
  6.5 377.6 %all-reduce.2.cloned.1.call-start = ((), (), s32[]{:S(2)}) async-start(), calls=%async_computation.1 | async-start | bytes 1048576 | tf_op jit(solution)/shard_map/psum | solution.py:118
  139.8 18.4 %copy-start.4 = (bf16[8,1024,128]{2,1,0:T(8,128)(2,1)S(1)}, bf16[8,1024,128]{2,1,0:T(8,128)(2,1)}, u32[]{:S(2)}) copy-start(bf16[8,1024,128]{2,1,0:T(8,128)(2,1)} %get-tuple-element.212) | copy-start | bytes 6291460
  157.7 5.0 %copy-start = (bf16[1024,1024]{1,0:T(8,128)(2,1)}, bf16[1024,1024]{1,0:T(8,128)(2,1)S(1)}, u32[]{:S(2)}) copy-start(bf16[1024,1024]{1,0:T(8,128)(2,1)S(1)} %get-tuple-element.276) | copy-start | bytes 6291460
  157.8 5.0 %copy-start.1 = (bf16[1024,1024]{1,0:T(8,128)(2,1)}, bf16[1024,1024]{1,0:T(8,128)(2,1)S(1)}, u32[]{:S(2)}) copy-start(bf16[1024,1024]{1,0:T(8,128)(2,1)S(1)} %get-tuple-element.277) | copy-start | bytes 6291460
  158.1 4.6 %copy-start.2 = (f32[1024]{0:T(1024)S(1)}, f32[1024]{0:T(1024)}, u32[]{:S(2)}) copy-start(f32[1024]{0:T(1024)} %param.14) | copy-start | bytes 12292
  256.2 6.6 %copy-start.3 = (f32[1024]{0:T(1024)S(1)}, f32[1024]{0:T(1024)}, u32[]{:S(2)}) copy-start(f32[1024]{0:T(1024)} %param.15) | copy-start | bytes 12292
Sparse Core Ops, SparseCore 0:
  265.0 119.1 all-reduce.1
where the time goes:
time: 392 us; the launch traced here: 393 us
  waiting for transfers between devices  119 us (30%)
  matrix products  93.8 us (24%)
  blocking collectives  60.9 us (16%)
  local copies, waits for them, and re-layouts  52 us (13%)
  other arithmetic  47.2 us (12%)
  between operations  13.5 us (3%)
  loops' own time  5.76 us (1%)
    psum x1, waiting for transfers between devices, per_device(): everything = lax.psum(partial_rows, 'row')  119 us
    dot_general x22, matrix products, add_block(): lax.dot_general(kernel_u, weighted, (((0,), (0,)), ((), ())), preferred_e...  82.7 us
    all_to_all x1, blocking collectives, per_device(): lax.all_to_all(columns, 'col', split_axis=2, concat_axis=3, tiled=True)  60.9 us
    convert_element_type x1, other arithmetic, dft_tables(): jnp.cos(angles).astype(jnp.bfloat16)  18 us
    unnamed x12, local copies, waits for them, and re-layouts  13.7 us
    all_to_all x2, local copies, waits for them, and re-layouts, per_device(): lax.all_to_all(columns, 'col', split_axis=2, concat_axis=3, tiled=True)  12.3 us
    mul x22, other arithmetic, add_block(): vis_part[1] * live_mask  12.1 us
    dynamic_slice x8, local copies, waits for them, and re-layouts, grid_slab(): return lax.map(one_subgrid, (visibility, baseline_uv, counts))  9.66 us
  transfers between devices with their start and end apart: 1, of which 1 were waited for; matrix products, arithmetic and copies ran while one was open for 0% of the time, Pallas kernels for 0%

commit v1 on v0

v1 whole, which is shorter than its diff:
```python
import functools
import math

import jax
import jax.numpy as jnp
import numpy as np
from jax import lax
from jax.experimental import pallas as pl
from jax.experimental.pallas import tpu as pltpu
from jax.sharding import PartitionSpec as P

IMAGE = 32768
SIDE = 1024
HALF = SIDE // 2
STRIDE = IMAGE // SIDE - 1
OWN = 4
ROWS = 128
MESH = pl.DeviceIdType.MESH

COS_POLY = (
    0.9999999890588229,
    -19.73920449945383,
    64.93911745989081,
    -85.45013953079767,
    60.167630950263465,
    -25.967599245923743,
    6.52865815775625,
)


def cos_turns(turns):
    frac = turns - jnp.round(turns)
    square = frac * frac
    value = COS_POLY[6] * square + COS_POLY[5]
    for factor in COS_POLY[4::-1]:
        value = value * square + factor
    return value


def half_table():
    pixel = STRIDE * np.arange(SIDE, dtype=np.int64) - IMAGE // 2
    odd = 2 * np.arange(HALF, dtype=np.int64) + 1
    angle = (2.0 * np.pi / (2 * IMAGE)) * np.mod(pixel[:, None] * odd[None, :], 2 * IMAGE)
    return np.concatenate([np.cos(angle), np.sin(angle)], axis=1).astype(jnp.bfloat16)


def chains(coord, emit):
    row = lax.broadcasted_iota(jnp.int32, (32, 128), 0).astype(jnp.float32)
    here = jnp.broadcast_to(coord, (32, 128))
    near = row - here
    up_mult = -2.0 * cos_turns(near * (1.0 / 32.0))
    down_mult = -2.0 * cos_turns((row + here + 1.0) * (1.0 / 32.0))

    def up_at(block):
        dist = near + float(HALF + 32 * block)
        return cos_turns(dist * dist * (1.0 / (2 * SIDE)))

    def down_at(block):
        dist = (row + here) - float(HALF - 1 - 32 * block)
        return cos_turns(dist * dist * (1.0 / (2 * SIDE)))

    up = [up_at(7), up_at(8)]
    down = [down_at(7), down_at(8)]
    emit(7, up[0], down[0])
    emit(8, up[1], down[1])
    after_up, before_up = up[1], up[0]
    after_down, before_down = down[1], down[0]
    for block in range(9, 16):
        after_up, before_up = up_mult * after_up - before_up, after_up
        after_down, before_down = down_mult * after_down - before_down, after_down
        emit(block, after_up, after_down)
    after_up, before_up = up[0], up[1]
    after_down, before_down = down[0], down[1]
    for block in range(6, -1, -1):
        after_up, before_up = up_mult * after_up - before_up, after_up
        after_down, before_down = down_mult * after_down - before_down, after_down
        emit(block, after_up, after_down)


def kernel(
    visibility,
    baseline,
    offsets,
    counts,
    taper_x,
    taper_y,
    table_hbm,
    result,
    table,
    even,
    odd,
    upper,
    lower,
    weighted,
    weights,
    phases,
    phase_u,
    kept,
    to_partner,
    from_partner,
    blocks,
    slots,
    table_sem,
    pair_send,
    pair_recv,
    block_send,
    block_recv,
):
    col = lax.axis_index("col")
    row = lax.axis_index("row")
    core = lax.rem(col, 2)
    plane = col // 2
    partner = col + 1 - 2 * core
    here_x = row // 4
    here_y = lax.rem(row, 4)

    load_table = pltpu.make_async_copy(table_hbm, table, table_sem)
    load_table.start()

    barrier = pltpu.get_barrier_semaphore()
    pl.semaphore_signal(barrier, inc=1, device_id={"col": partner, "row": row}, device_id_type=MESH)
    for step in range(1, 16):
        other = lax.rem(row + step, 16)
        pl.semaphore_signal(barrier, inc=1, device_id={"col": col, "row": other}, device_id_type=MESH)

    pixel = STRIDE * lax.broadcasted_iota(jnp.int32, (8, SIDE), 1) - IMAGE // 2
    scale = 4.0 / (SIDE * math.sqrt(float(128 * SIDE)))
    parts = []
    for axis, taper, factor in ((0, taper_x, 1.0), (1, taper_y, scale)):
        shift = 2 * offsets[:, axis : axis + 1] + (SIDE - 1)
        turns = (pixel * shift) & (2 * IMAGE - 1)
        frac = turns.astype(jnp.float32) * (1.0 / (2 * IMAGE))
        size = jnp.broadcast_to(taper[...] * factor, (8, SIDE))
        parts.append(size * cos_turns(frac))
        parts.append(size * cos_turns(frac - 0.25))
    first = core == 0
    own_parts = [jnp.where(first, part[0:4], part[4:8]) for part in parts]
    square = jnp.concatenate(own_parts + [jnp.zeros((ROWS - 16, SIDE), jnp.float32)], axis=0)
    phases[...] = square.T

    own_first = pl.multiple_of(plane * ROWS + core * 64, 64)
    other_first = pl.multiple_of(plane * ROWS + (1 - core) * 64, 64)
    for near, place in ((0, own_first), (1, other_first)):
        some = phases[pl.ds(place, 64), :]
        for sub in range(OWN):
            for part in range(2):
                column = some[:, 4 * part + sub : 4 * part + sub + 1]
                phase_u[sub, part, near] = jnp.broadcast_to(column, (64, 128))

    load_table.wait()

    def one_subgrid(sub, carry):
        which = core * OWN + sub
        live = counts[which]

        def fill_u(block, inner):
            lanes = pl.ds(pl.multiple_of(block * 128, 128), 128)

            def emit(at, up, down):
                even[pl.ds(32 * at, 32), lanes] = (up + down).astype(jnp.bfloat16)
                odd[pl.ds(32 * at, 32), lanes] = (up - down).astype(jnp.bfloat16)

            chains(baseline[which, 0:1, lanes], emit)
            return inner

        lax.fori_loop(0, 8, fill_u, 0)

        def fill_v(block, inner):
            lanes = pl.ds(pl.multiple_of(block * 128, 128), 128)

            def emit(at, up, down):
                upper[pl.ds(32 * at, 32), lanes] = up.astype(jnp.bfloat16)
                lower[pl.ds(32 * at, 32), lanes] = down.astype(jnp.bfloat16)

            chains(baseline[which, 1:2, lanes], emit)
            return inner

        lax.fori_loop(0, 8, fill_v, 0)

        for near, place in ((0, own_first), (1, other_first)):
            cos_rows = table[pl.ds(place, 64), 0:HALF]
            sin_rows = table[pl.ds(place, 64), HALF:SIDE]
            for block in range(4):
                lanes = slice(256 * block, 256 * block + 256)
                real = jnp.dot(cos_rows, even[:, lanes], preferred_element_type=jnp.float32)
                imag = jnp.dot(sin_rows, odd[:, lanes], preferred_element_type=jnp.float32)
                mask = lax.broadcasted_iota(jnp.int32, (1, 256), 1) + 256 * block < live
                vis_re = jnp.where(mask, visibility[which, 0:1, lanes], 0.0)
                vis_im = jnp.where(mask, visibility[which, 1:2, lanes], 0.0)
                mid_re = real * vis_re - imag * vis_im
                mid_im = real * vis_im + imag * vis_re
                turn_re = jnp.concatenate([phase_u[sub, 0, near]] * 2, axis=1)
                turn_im = jnp.concatenate([phase_u[sub, 1, near]] * 2, axis=1)
                out_re = mid_re * turn_re - mid_im * turn_im
                out_im = mid_re * turn_im + mid_im * turn_re
                weighted[128 * near : 128 * near + 64, lanes] = out_re.astype(jnp.bfloat16)
                weighted[128 * near + 64 : 128 * near + 128, lanes] = out_im.astype(jnp.bfloat16)

        sign = jnp.where(lax.broadcasted_iota(jnp.int32, (128, 128), 1) < 64, -1.0, 1.0)

        def gather_k(tile, inner):
            at = pl.ds(pl.multiple_of(tile * 128, 128), 128)
            contract = (((1,), (1,)), ((), ()))
            plus = lax.dot_general(
                upper[at, :], weighted[...], contract, preferred_element_type=jnp.float32
            )
            minus = lax.dot_general(
                lower[at, :], weighted[...], contract, preferred_element_type=jnp.float32
            )
            weights[sub, at, :] = (plus + minus).astype(jnp.bfloat16)
            diff = plus - minus
            at_odd = pl.ds(pl.multiple_of(HALF + tile * 128, 128), 128)
            for near in range(2):
                turned = pltpu.roll(diff[:, 128 * near : 128 * near + 128], 64, 1) * sign
                weights[sub, at_odd, 128 * near : 128 * near + 128] = turned.astype(jnp.bfloat16)
            return inner

        lax.fori_loop(0, 4, gather_k, 0)
        return carry

    lax.fori_loop(0, OWN, one_subgrid, 0)

    sign_row = jnp.where(lax.broadcasted_iota(jnp.int32, (256, 128), 1) < 64, -1.0, 1.0)

    def pair_copy(step):
        return pltpu.make_async_remote_copy(
            src_ref=to_partner.at[step],
            dst_ref=from_partner.at[step],
            send_sem=pair_send.at[step],
            recv_sem=pair_recv.at[step],
            device_id={"col": partner, "row": row},
            device_id_type=MESH,
        )

    def block_copy(step, hop):
        to_x = lax.rem(here_x + 3 - step, 4)
        to_y = lax.rem(here_y + hop, 4)
        return pltpu.make_async_remote_copy(
            src_ref=blocks.at[step, hop],
            dst_ref=slots.at[step, hop],
            send_sem=block_send.at[step, hop],
            recv_sem=block_recv.at[step, hop],
            device_id={"col": col, "row": to_x * 4 + to_y},
            device_id_type=MESH,
        )

    def transform(step):
        to_x = lax.rem(here_x + 3 - step, 4)
        place = pl.ds(pl.multiple_of(to_x * 256, 256), 256)
        lhs = table[place, :]
        columns = phases[place, :]
        sums = [jnp.zeros((256, 128), jnp.float32)] * 2
        for sub in range(OWN):
            product = jnp.dot(lhs, weights[sub], preferred_element_type=jnp.float32)
            turn_re = jnp.broadcast_to(columns[:, 8 + sub : 9 + sub], (256, 128))
            turn_im = jnp.broadcast_to(columns[:, 12 + sub : 13 + sub], (256, 128)) * sign_row
            for near in range(2):
                part = product[:, 128 * near : 128 * near + 128]
                sums[near] = sums[near] + (part * turn_re + pltpu.roll(part, 64, 1) * turn_im)
        kept[step] = sums[0]
        to_partner[step] = sums[1].astype(jnp.bfloat16)

    def finish(step):
        pair_copy(step).wait_recv()
        both = kept[step] + from_partner[step].astype(jnp.float32)
        kept[step] = both
        for hop in range(4):
            to_y = lax.rem(here_y + hop, 4)
            if step == 3 and hop == 0:
                continue
            piece = kept[step, pl.ds(pl.multiple_of(to_y * 64, 64), 64), :]
            blocks[step, hop] = piece.astype(jnp.bfloat16)
            block_copy(step, hop).start()

    for step in range(4):
        transform(step)
        if step == 0:
            pl.semaphore_wait(barrier, 16)
        pair_copy(step).start()
        if step > 0:
            finish(step - 1)
    finish(3)

    total = kept[3, pl.ds(pl.multiple_of(here_y * 64, 64), 64), :]
    for step in range(4):
        for hop in range(4):
            if step == 3 and hop == 0:
                continue
            block_copy(step, hop).wait_recv()
            total = total + slots[step, hop].astype(jnp.float32)
    result[...] = total
    for step in range(4):
        pair_copy(step).wait_send()
        for hop in range(4):
            if step == 3 and hop == 0:
                continue
            block_copy(step, hop).wait_send()


def per_device(visibility, baseline, offsets, counts, taper_x, taper_y):
    vmem = pl.BlockSpec(memory_space=pltpu.VMEM)
    smem = pl.BlockSpec(memory_space=pltpu.SMEM)
    half = jnp.bfloat16
    full = jnp.float32
    total = pl.pallas_call(
        kernel,
        out_shape=jax.ShapeDtypeStruct((64, 128), full),
        in_specs=[vmem, vmem, vmem, smem, vmem, vmem, pl.BlockSpec(memory_space=pl.ANY)],
        out_specs=vmem,
        scratch_shapes=[
            pltpu.VMEM((SIDE, SIDE), half),
            pltpu.VMEM((HALF, SIDE), half),
            pltpu.VMEM((HALF, SIDE), half),
            pltpu.VMEM((HALF, SIDE), half),
            pltpu.VMEM((HALF, SIDE), half),
            pltpu.VMEM((2 * ROWS, SIDE), half),
            pltpu.VMEM((OWN, SIDE, 2 * ROWS), half),
            pltpu.VMEM((SIDE, 128), full),
            pltpu.VMEM((OWN, 2, 2, 64, 128), full),
            pltpu.VMEM((4, 256, 128), full),
            pltpu.VMEM((4, 256, 128), half),
            pltpu.VMEM((4, 256, 128), half),
            pltpu.VMEM((4, 4, 64, 128), half),
            pltpu.VMEM((4, 4, 64, 128), half),
            pltpu.SemaphoreType.DMA,
            pltpu.SemaphoreType.DMA((4,)),
            pltpu.SemaphoreType.DMA((4,)),
            pltpu.SemaphoreType.DMA((4, 4)),
            pltpu.SemaphoreType.DMA((4, 4)),
        ],
        compiler_params=pltpu.CompilerParams(
            collective_id=0, has_side_effects=True, vmem_limit_bytes=40 * 1024 * 1024
        ),
        name="facet_rows",
    )(
        visibility,
        baseline,
        offsets,
        counts,
        taper_x.reshape(1, SIDE),
        taper_y.reshape(1, SIDE),
        jnp.asarray(half_table()),
    )
    return total.T.reshape(2, 64, 64)


def solution(mesh):
    placed = (P("row", None, None), P("row", None, None), P("row", None), P("row"), P(), P())
    return jax.shard_map(
        per_device, mesh=mesh, in_specs=placed, out_specs=P(None, "col", "row"), check_vma=False
    )
```

time: 392 us -> 43.2 us (0.11)
  waiting for transfers between devices: 119 us -> 0 us
  matrix products: 93.8 us -> 0 us
  blocking collectives: 60.9 us -> 0 us
  other arithmetic: 47.2 us -> 0 us
  local copies, waits for them, and re-layouts: 52 us -> 6.78 us
  Pallas kernels: 0 us -> 36.1 us
  between operations: 13.5 us -> 0.02 us
  loops' own time: 5.76 us -> 0 us
    psum x1 -> x0, waiting for transfers between devices: 119 us -> none  [per_device(): everything = lax.psum(partial_rows, 'row')]
    dot_general x24 -> x0, matrix products: 93.8 us -> none  [the longest x22 82.7 us: add_block(): lax.dot_general(kernel_u, weighted, (((0,), (0,)), ((), ())), preferred_e...]
    all_to_all x1 -> x0, blocking collectives: 60.9 us -> none  [per_device(): lax.all_to_all(columns, 'col', split_axis=2, concat_axis=3, tiled=True)]
    pallas_call x0 -> x1, Pallas kernels: none -> 36.1 us  [per_device(): pl.pallas_call(kernel, out_shape=jax.ShapeDtypeStruct((64, 128), full), i...]
    convert_element_type x1 -> x0, other arithmetic: 18 us -> none  [dft_tables(): jnp.cos(angles).astype(jnp.bfloat16)]
    mul x23 -> x0, other arithmetic: 13 us -> none  [the longest x22 12.1 us: add_block(): vis_part[1] * live_mask]
    all_to_all x2 -> x0, local copies, waits for them, and re-layouts: 12.3 us -> none  [per_device(): lax.all_to_all(columns, 'col', split_axis=2, concat_axis=3, tiled=True)]
    dynamic_slice x9 -> x0, local copies, waits for them, and re-layouts: 11.2 us -> none  [the longest x8 9.66 us: grid_slab(): return lax.map(one_subgrid, (visibility, baseline_uv, counts))]
  transfers between devices with their start and end apart: 1 -> 0, of which waited for: 1 -> 0; matrix products, arithmetic and copies ran while one was open for 0% -> 0% of each run, Pallas kernels for 0% -> 0%
where the time goes in v1:
time: 43.2 us; the launch traced here: 42.9 us
  Pallas kernels  36.1 us (84%)
  local copies, waits for them, and re-layouts  6.78 us (16%)
    pallas_call x1, Pallas kernels, per_device(): pl.pallas_call(kernel, out_shape=jax.ShapeDtypeStruct((64, 128), full), i...  36.1 us
    unnamed x13, local copies, waits for them, and re-layouts  6.05 us

profile of v1, /device:TPU:1, one launch (start us, length us, event | category | flops | bytes accessed | tf_op | source)
XLA Modules:
  0.0 42.9 jit_solution(11547745454059797897)
XLA Ops:
  0.0 0.8 %copy.8.offsets = s32[8,2]{1,0:T(8,128)S(1)} copy(s32[8,2]{0,1:T(2,128)} %param.9) | data formatting | bytes 128 | tf_op args[2]
  0.8 0.0 copy-start
  0.8 1.6 %copy-done = bf16[1024,1024]{1,0:T(8,128)(2,1)S(1)} copy-done((bf16[1024,1024]{1,0:T(8,128)(2,1)S(1)}, bf16[1024,1024]{1,0:T(8,128)(2,1)}, u32[]{:S(2)}) %copy-start) | copy-done | bytes 2097176
  2.3 0.0 copy-start.1
  2.3 0.8 %copy-done.1 = f32[8,2,1024]{2,1,0:T(2,128)S(1)} copy-done((f32[8,2,1024]{2,1,0:T(2,128)S(1)}, f32[8,2,1024]{2,1,0:T(2,128)}, u32[]{:S(2)}) %copy-start.1) | copy-done | bytes 65560
  3.2 0.0 copy-start.2
  3.2 0.8 %copy-done.2 = f32[8,2,1024]{2,1,0:T(2,128)S(1)} copy-done((f32[8,2,1024]{2,1,0:T(2,128)S(1)}, f32[8,2,1024]{2,1,0:T(2,128)}, u32[]{:S(2)}) %copy-start.2) | copy-done | bytes 65560
  4.0 0.0 copy-start.3
  4.0 0.7 %copy-done.3 = f32[1024]{0:T(1024)S(1)} copy-done((f32[1024]{0:T(1024)S(1)}, f32[1024]{0:T(1024)}, u32[]{:S(2)}) %copy-start.3) | copy-done | bytes 4120
  4.7 0.0 copy-start.4
  4.7 0.7 %copy-done.4 = f32[1024]{0:T(1024)S(1)} copy-done((f32[1024]{0:T(1024)S(1)}, f32[1024]{0:T(1024)}, u32[]{:S(2)}) %copy-start.4) | copy-done | bytes 4120
  5.4 0.0 copy-start.5
  5.4 0.7 %copy-done.5 = s32[8]{0:T(128)S(1)} copy-done((s32[8]{0:T(128)S(1)}, s32[8]{0:T(128)}, u32[]{:S(2)}) %copy-start.5) | copy-done | bytes 56
  6.1 36.1 %facet_rows.1 = f32[64,128]{1,0:T(8,128)S(1)} custom-call(f32[8,2,1024]{2,1,0:T(2,128)S(1)} %copy-done.1, f32[8,2,1024]{2,1,0:T(2,128)S(1)} %copy-done.2, s32[8,2]{1,0:T(8,128)S(1)} %copy.8.offsets, s32[8]{0:T(128)S(1)} %copy-done.5, f32[1,1024]{1,0:T(1,128)S(1)} %bitcast.5, f32[1,1024]{1,0:T(1,128)S(1)} %bitcast.6, bf16[1024,1024]{1,0:T(8,128)(2,1)S(1)} %copy-done), custom_call_target="tpu_custom_call" | custom-call | tf_op jit(solution)/shard_map/facet_rows/pallas_call | solution.py:305
  42.2 0.7 %copy.10 = f32[128,64]{1,0:T(8,128)} copy(f32[128,64]{0,1:T(8,128)S(1)} %bitcast.4) | data formatting | bytes 65536 | tf_op jit(solution)/shard_map/reshape | solution.py:344
Async XLA Ops:
  0.8 1.6 %copy-start = (bf16[1024,1024]{1,0:T(8,128)(2,1)S(1)}, bf16[1024,1024]{1,0:T(8,128)(2,1)}, u32[]{:S(2)}) copy-start(bf16[1024,1024]{1,0:T(8,128)(2,1)} %constant.2.clone.table_hbm) | copy-start | bytes 6291460
  2.3 0.8 %copy-start.1 = (f32[8,2,1024]{2,1,0:T(2,128)S(1)}, f32[8,2,1024]{2,1,0:T(2,128)}, u32[]{:S(2)}) copy-start(f32[8,2,1024]{2,1,0:T(2,128)} %visibility.1) | copy-start | bytes 196612
  3.2 0.8 %copy-start.2 = (f32[8,2,1024]{2,1,0:T(2,128)S(1)}, f32[8,2,1024]{2,1,0:T(2,128)}, u32[]{:S(2)}) copy-start(f32[8,2,1024]{2,1,0:T(2,128)} %baseline.1) | copy-start | bytes 196612
  4.0 0.7 %copy-start.3 = (f32[1024]{0:T(1024)S(1)}, f32[1024]{0:T(1024)}, u32[]{:S(2)}) copy-start(f32[1024]{0:T(1024)} %param.11) | copy-start | bytes 12292
  4.7 0.7 %copy-start.4 = (f32[1024]{0:T(1024)S(1)}, f32[1024]{0:T(1024)}, u32[]{:S(2)}) copy-start(f32[1024]{0:T(1024)} %param.12) | copy-start | bytes 12292
  5.4 0.7 %copy-start.5 = (s32[8]{0:T(128)S(1)}, s32[8]{0:T(128)}, u32[]{:S(2)}) copy-start(s32[8]{0:T(128)} %counts.1) | copy-start | bytes 100

commit v2 on v1

v2 whole, which is shorter than its diff:
```python
import functools
import math

import jax
import jax.numpy as jnp
import numpy as np
from jax import lax
from jax.experimental import pallas as pl
from jax.experimental.pallas import tpu as pltpu
from jax.sharding import PartitionSpec as P

IMAGE = 32768
SIDE = 1024
HALF = SIDE // 2
STRIDE = IMAGE // SIDE - 1
OWN = 4
ROWS = 128
MESH = pl.DeviceIdType.MESH

COS_POLY = (
    0.9999999890588229,
    -19.73920449945383,
    64.93911745989081,
    -85.45013953079767,
    60.167630950263465,
    -25.967599245923743,
    6.52865815775625,
)


def cos_turns(turns):
    frac = turns - jnp.round(turns)
    square = frac * frac
    value = COS_POLY[6] * square + COS_POLY[5]
    for factor in COS_POLY[4::-1]:
        value = value * square + factor
    return value


def half_table():
    pixel = STRIDE * np.arange(SIDE, dtype=np.int64) - IMAGE // 2
    odd = 2 * np.arange(HALF, dtype=np.int64) + 1
    angle = (2.0 * np.pi / (2 * IMAGE)) * np.mod(pixel[:, None] * odd[None, :], 2 * IMAGE)
    return np.concatenate([np.cos(angle), np.sin(angle)], axis=1).astype(jnp.bfloat16)


def chains(coord, turns, emit):
    row = lax.broadcasted_iota(jnp.int32, (32, 128), 0).astype(jnp.float32)
    near = row - jnp.broadcast_to(coord, (32, 128))
    small = jnp.broadcast_to(coord * (1.0 / 32.0), (8, 128))
    cos_here = jnp.concatenate([cos_turns(small)] * 4, axis=0)
    sin_here = jnp.concatenate([cos_turns(small - 0.25)] * 4, axis=0)
    multiplier = turns[0:32] * cos_here + turns[32:64] * sin_here

    def anchor(block):
        dist = near + float(32 * block)
        return cos_turns(dist * dist * (1.0 / (2 * SIDE)))

    flip = 7 - lax.broadcasted_iota(jnp.int32, (8, 128), 0)

    def reverse(block):
        pieces = [block[8 * i : 8 * i + 8] for i in range(3, -1, -1)]
        return jnp.concatenate([jnp.take_along_axis(p, flip, axis=0) for p in pieces], axis=0)

    below, above = anchor(15), anchor(16)
    starts = ((multiplier, below, above), tuple(map(reverse, (multiplier, above, below))))
    for part, (factor, before, now) in enumerate(starts):
        for block in range(16):
            emit(part, block, now)
            if block < 15:
                now, before = factor * now - before, now


def kernel(
    visibility_hbm,
    baseline_hbm,
    offsets_hbm,
    counts_hbm,
    taper_x_hbm,
    taper_y_hbm,
    table_hbm,
    result,
    visibility,
    baseline,
    offsets,
    counts,
    taper,
    table,
    own_table,
    turns,
    grid_u,
    grid_v,
    weighted,
    weights,
    phases,
    phase_u,
    kept,
    to_partner,
    from_partner,
    blocks,
    slots,
    load_sem,
    pair_send,
    pair_recv,
    block_send,
    block_recv,
):
    col = lax.axis_index("col")
    row = lax.axis_index("row")
    core = lax.rem(col, 2)
    plane = col // 2
    partner = col + 1 - 2 * core
    here_x = row // 4
    here_y = lax.rem(row, 4)

    own = pl.ds(core * OWN, OWN)
    loads = [
        pltpu.make_async_copy(baseline_hbm.at[own], baseline, load_sem.at[0]),
        pltpu.make_async_copy(offsets_hbm, offsets, load_sem.at[1]),
        pltpu.make_async_copy(taper_x_hbm, taper.at[0], load_sem.at[2]),
        pltpu.make_async_copy(taper_y_hbm, taper.at[1], load_sem.at[3]),
        pltpu.make_async_copy(counts_hbm, counts, load_sem.at[4]),
        pltpu.make_async_copy(visibility_hbm.at[own], visibility, load_sem.at[5]),
        pltpu.make_async_copy(table_hbm, table, load_sem.at[6]),
    ]
    for load in loads:
        load.start()

    barrier = pltpu.get_barrier_semaphore()
    pl.semaphore_signal(barrier, inc=1, device_id={"col": partner, "row": row}, device_id_type=MESH)
    for step in range(1, 16):
        other = lax.rem(row + step, 16)
        pl.semaphore_signal(barrier, inc=1, device_id={"col": col, "row": other}, device_id_type=MESH)

    circle = lax.broadcasted_iota(jnp.int32, (32, 128), 0).astype(jnp.float32) * (1.0 / 32.0)
    turns[0:32] = -2.0 * cos_turns(circle)
    turns[32:64] = -2.0 * cos_turns(circle - 0.25)

    def fill_u(sub, block):
        def emit(part, at, value):
            grid_u[block, HALF * part + 32 * at : HALF * part + 32 * at + 32] = value.astype(jnp.bfloat16)

        lanes = pl.ds(block * 128, 128) if isinstance(block, int) else pl.ds(pl.multiple_of(block * 128, 128), 128)
        chains(baseline[sub, 0:1, lanes], turns, emit)

    def fill_v(sub, block):
        def emit(part, at, value):
            first = 256 * (at // 4) + 128 * part + 32 * (at % 4)
            grid_v[block, first : first + 32] = value.astype(jnp.bfloat16)

        lanes = pl.ds(block * 128, 128) if isinstance(block, int) else pl.ds(pl.multiple_of(block * 128, 128), 128)
        chains(baseline[sub, 1:2, lanes], turns, emit)

    for load in loads[:4]:
        load.wait()

    def first_fill(block, inner):
        fill_u(0, block)
        return inner

    lax.fori_loop(0, 8, first_fill, 0)

    pixel = STRIDE * lax.broadcasted_iota(jnp.int32, (8, SIDE), 1) - IMAGE // 2
    subgrid = lax.broadcasted_iota(jnp.int32, (8, SIDE), 0)
    scale = 4.0 / (SIDE * math.sqrt(float(128 * SIDE)))
    parts = []
    for axis, factor in ((0, 1.0), (1, scale)):
        shift = jnp.zeros((8, SIDE), jnp.int32)
        for sub in range(OWN):
            shift = jnp.where(subgrid == sub, 2 * offsets[axis, core * OWN + sub] + (SIDE - 1), shift)
        frac = ((pixel * shift) & (2 * IMAGE - 1)).astype(jnp.float32) * (1.0 / (2 * IMAGE))
        size = jnp.broadcast_to(taper[axis] * factor, (8, SIDE))
        parts.append(size * cos_turns(frac))
        parts.append(size * cos_turns(frac - 0.25))
    square = jnp.concatenate(parts + [jnp.zeros((ROWS - 32, SIDE), jnp.float32)], axis=0)
    phases[...] = square.T

    for load in loads[4:]:
        load.wait()

    for near in range(2):
        place = pl.multiple_of(plane * ROWS + (core if near == 0 else 1 - core) * 64, 64)
        some = phases[pl.ds(place, 64), :]
        for sub in range(OWN):
            for part in range(2):
                column = some[:, 8 * part + sub : 8 * part + sub + 1]
                phase_u[sub, near, part] = jnp.broadcast_to(column, (64, 128))
        cos_rows = table[pl.ds(place, 64), 0:HALF]
        sin_rows = table[pl.ds(place, 64), HALF:SIDE]
        own_table[128 * near : 128 * near + 64, 0:HALF] = cos_rows
        own_table[128 * near : 128 * near + 64, HALF:SIDE] = cos_rows
        own_table[128 * near + 64 : 128 * near + 128, 0:HALF] = sin_rows
        own_table[128 * near + 64 : 128 * near + 128, HALF:SIDE] = -sin_rows

    slot = lax.broadcasted_iota(jnp.int32, (2, SIDE), 1)
    for sub in range(OWN):
        mask = slot < counts[core * OWN + sub]
        visibility[sub] = jnp.where(mask, visibility[sub], 0.0)

    def rows_of_image(sub, step):
        rhs = jnp.concatenate([grid_u[2 * step], grid_u[2 * step + 1]], axis=1)
        product = jnp.dot(own_table[...], rhs, preferred_element_type=jnp.float32)
        lanes = pl.ds(step * 256, 256)
        vis_re = visibility[sub, 0:1, lanes]
        vis_im = visibility[sub, 1:2, lanes]
        for near in range(2):
            real = product[128 * near : 128 * near + 64]
            imag = product[128 * near + 64 : 128 * near + 128]
            mid_re = real * vis_re - imag * vis_im
            mid_im = real * vis_im + imag * vis_re
            turn_re = jnp.concatenate([phase_u[sub, near, 0]] * 2, axis=1)
            turn_im = jnp.concatenate([phase_u[sub, near, 1]] * 2, axis=1)
            out_re = mid_re * turn_re - mid_im * turn_im
            out_im = mid_re * turn_im + mid_im * turn_re
            both = jnp.concatenate([out_re, out_im], axis=0).astype(jnp.bfloat16)
            weighted[near, lanes, :] = both.T

    sign = jnp.where(lax.broadcasted_iota(jnp.int32, (128, 128), 1) < 64, -1.0, 1.0)

    def columns_of_grid(sub, step):
        place = pl.ds(step * 256, 256)
        lhs = jnp.concatenate([grid_v[i, place, :] for i in range(8)], axis=1)
        rhs = jnp.concatenate([weighted[0], weighted[1]], axis=1)
        product = jnp.dot(lhs, rhs, preferred_element_type=jnp.float32)
        plus, minus = product[0:128], product[128:256]
        at = pl.ds(step * 128, 128)
        at_odd = pl.ds(HALF + step * 128, 128)
        total = (plus + minus).astype(jnp.bfloat16)
        diff = plus - minus
        for near in range(2):
            lanes = slice(128 * near, 128 * near + 128)
            weights[sub, near, at, :] = total[:, lanes]
            weights[sub, near, at_odd, :] = (pltpu.roll(diff[:, lanes], 64, 1) * sign).astype(jnp.bfloat16)

    def one_subgrid(sub, carry):
        def first_half(step, inner):
            rows_of_image(sub, step)
            fill_v(sub, 2 * step)
            fill_v(sub, 2 * step + 1)
            return inner

        def second_half(step, inner):
            columns_of_grid(sub, step)
            fill_u(jnp.minimum(sub + 1, OWN - 1), 2 * step)
            fill_u(jnp.minimum(sub + 1, OWN - 1), 2 * step + 1)
            return inner

        for step in range(4):
            first_half(step, 0)
        for step in range(4):
            second_half(step, 0)
        return carry

    lax.fori_loop(0, OWN, one_subgrid, 0)

    sign_row = jnp.where(lax.broadcasted_iota(jnp.int32, (256, 128), 1) < 64, -1.0, 1.0)

    def pair_copy(step):
        return pltpu.make_async_remote_copy(
            src_ref=to_partner.at[step],
            dst_ref=from_partner.at[step],
            send_sem=pair_send.at[step],
            recv_sem=pair_recv.at[step],
            device_id={"col": partner, "row": row},
            device_id_type=MESH,
        )

    def block_copy(step, hop):
        to_x = lax.rem(here_x + 3 - step, 4)
        to_y = lax.rem(here_y + hop, 4)
        return pltpu.make_async_remote_copy(
            src_ref=blocks.at[step, hop],
            dst_ref=slots.at[step, hop],
            send_sem=block_send.at[step, hop],
            recv_sem=block_recv.at[step, hop],
            device_id={"col": col, "row": to_x * 4 + to_y},
            device_id_type=MESH,
        )

    def transform(step):
        to_x = lax.rem(here_x + 3 - step, 4)
        place = pl.ds(pl.multiple_of(to_x * 256, 256), 256)
        lhs = table[place, :]
        columns = phases[place, :]
        sums = [jnp.zeros((256, 128), jnp.float32)] * 2
        for sub in range(OWN):
            rhs = jnp.concatenate([weights[sub, 0], weights[sub, 1]], axis=1)
            product = jnp.dot(lhs, rhs, preferred_element_type=jnp.float32)
            turn_re = jnp.broadcast_to(columns[:, 16 + sub : 17 + sub], (256, 128))
            turn_im = jnp.broadcast_to(columns[:, 24 + sub : 25 + sub], (256, 128)) * sign_row
            for near in range(2):
                part = product[:, 128 * near : 128 * near + 128]
                sums[near] = sums[near] + (part * turn_re + pltpu.roll(part, 64, 1) * turn_im)
        kept[step] = sums[0]
        to_partner[step] = sums[1].astype(jnp.bfloat16)

    def finish(step):
        pair_copy(step).wait_recv()
        both = kept[step] + from_partner[step].astype(jnp.float32)
        kept[step] = both
        for hop in range(4):
            to_y = lax.rem(here_y + hop, 4)
            if step == 3 and hop == 0:
                continue
            piece = kept[step, pl.ds(pl.multiple_of(to_y * 64, 64), 64), :]
            blocks[step, hop] = piece.astype(jnp.bfloat16)
            block_copy(step, hop).start()

    for step in range(4):
        transform(step)
        if step == 0:
            pl.semaphore_wait(barrier, 16)
        pair_copy(step).start()
        if step > 0:
            finish(step - 1)
    finish(3)

    total = kept[3, pl.ds(pl.multiple_of(here_y * 64, 64), 64), :]
    for step in range(4):
        for hop in range(4):
            if step == 3 and hop == 0:
                continue
            block_copy(step, hop).wait_recv()
            total = total + slots[step, hop].astype(jnp.float32)
    result[...] = total
    for step in range(4):
        pair_copy(step).wait_send()
        for hop in range(4):
            if step == 3 and hop == 0:
                continue
            block_copy(step, hop).wait_send()


def per_device(visibility, baseline, offsets, counts, taper_x, taper_y):
    hbm = pl.BlockSpec(memory_space=pltpu.HBM)
    half = jnp.bfloat16
    full = jnp.float32
    total = pl.pallas_call(
        kernel,
        out_shape=jax.ShapeDtypeStruct((64, 128), full),
        in_specs=[hbm] * 7,
        out_specs=pl.BlockSpec(memory_space=pltpu.VMEM),
        scratch_shapes=[
            pltpu.VMEM((OWN, 2, SIDE), full),
            pltpu.VMEM((OWN, 2, SIDE), full),
            pltpu.SMEM((2, 8), jnp.int32),
            pltpu.SMEM((8,), jnp.int32),
            pltpu.VMEM((2, 1, SIDE), full),
            pltpu.VMEM((SIDE, SIDE), half),
            pltpu.VMEM((2 * ROWS, SIDE), half),
            pltpu.VMEM((64, 128), full),
            pltpu.VMEM((8, SIDE, 128), half),
            pltpu.VMEM((8, SIDE, 128), half),
            pltpu.VMEM((2, SIDE, 128), half),
            pltpu.VMEM((OWN, 2, SIDE, 128), half),
            pltpu.VMEM((SIDE, 128), full),
            pltpu.VMEM((OWN, 2, 2, 64, 128), full),
            pltpu.VMEM((4, 256, 128), full),
            pltpu.VMEM((4, 256, 128), half),
            pltpu.VMEM((4, 256, 128), half),
            pltpu.VMEM((4, 4, 64, 128), half),
            pltpu.VMEM((4, 4, 64, 128), half),
            pltpu.SemaphoreType.DMA((7,)),
            pltpu.SemaphoreType.DMA((4,)),
            pltpu.SemaphoreType.DMA((4,)),
            pltpu.SemaphoreType.DMA((4, 4)),
            pltpu.SemaphoreType.DMA((4, 4)),
        ],
        compiler_params=pltpu.CompilerParams(
            collective_id=0, has_side_effects=True, vmem_limit_bytes=67043328
        ),
        name="facet_rows",
    )(
        visibility,
        baseline,
        offsets.T,
        counts,
        taper_x.reshape(1, SIDE),
        taper_y.reshape(1, SIDE),
        jnp.asarray(half_table()),
    )
    return total.T.reshape(2, 64, 64)


def solution(mesh):
    placed = (P("row", None, None), P("row", None, None), P("row", None), P("row"), P(), P())
    return jax.shard_map(
        per_device, mesh=mesh, in_specs=placed, out_specs=P(None, "col", "row"), check_vma=False
    )
```

time: 43.2 us -> 26.9 us (0.62)
  Pallas kernels: 36.1 us -> 25.2 us
  local copies, waits for them, and re-layouts: 6.78 us -> 1.49 us
    pallas_call x1, Pallas kernels: 36.1 us -> 25.2 us  [per_device(): pl.pallas_call(kernel, out_shape=jax.ShapeDtypeStruct((64, 128), full), i...]
    unnamed x13 -> x0, local copies, waits for them, and re-layouts: 6.05 us -> none
    reshape x1, local copies, waits for them, and re-layouts: 0.73 us -> 1.49 us  [per_device(): return total.T.reshape(2, 64, 64)]
where the time goes in v2:
time: 26.9 us; the launch traced here: 26.7 us
  Pallas kernels  25.2 us (94%)
  local copies, waits for them, and re-layouts  1.49 us (6%)
    pallas_call x1, Pallas kernels, per_device(): pl.pallas_call(kernel, out_shape=jax.ShapeDtypeStruct((64, 128), full), i...  25.2 us
    reshape x1, local copies, waits for them, and re-layouts, per_device(): return total.T.reshape(2, 64, 64)  1.49 us

profile of v2, /device:TPU:1, one launch (start us, length us, event | category | flops | bytes accessed | tf_op | source)
XLA Modules:
  0.0 26.7 jit_solution(3038316376527954627)
XLA Ops:
  0.0 25.2 %facet_rows.1 = f32[64,128]{1,0:T(8,128)} custom-call(f32[8,2,1024]{2,1,0:T(2,128)} %visibility_hbm.1, f32[8,2,1024]{2,1,0:T(2,128)} %baseline_hbm.1, s32[2,8]{1,0:T(2,128)} %bitcast.8, s32[8]{0:T(128)} %counts_hbm.1, f32[1,1024]{1,0:T(1,128)} %bitcast.6, f32[1,1024]{1,0:T(1,128)} %bitcast.7, bf16[1024,1024]{1,0:T(8,128)(2,1)} %constant.2.clone.table_hbm), custom_call_target="tpu_custom_call" | custom-call | tf_op jit(solution)/shard_map/facet_rows/pallas_call | solution.py:338
  25.2 1.5 %copy.9 = f32[128,64]{1,0:T(8,128)} copy(f32[128,64]{0,1:T(8,128)} %bitcast.5) | data formatting | bytes 65536 | tf_op jit(solution)/shard_map/reshape | solution.py:382

commit v3 on v2

--- a/solution.py
+++ b/solution.py
@@ -44,12 +44,9 @@
     return np.concatenate([np.cos(angle), np.sin(angle)], axis=1).astype(jnp.bfloat16)
 
 
-def chains(coord, turns, emit):
+def chains(coord, cos_here, sin_here, turns, emit):
     row = lax.broadcasted_iota(jnp.int32, (32, 128), 0).astype(jnp.float32)
     near = row - jnp.broadcast_to(coord, (32, 128))
-    small = jnp.broadcast_to(coord * (1.0 / 32.0), (8, 128))
-    cos_here = jnp.concatenate([cos_turns(small)] * 4, axis=0)
-    sin_here = jnp.concatenate([cos_turns(small - 0.25)] * 4, axis=0)
     multiplier = turns[0:32] * cos_here + turns[32:64] * sin_here
 
     def anchor(block):
@@ -88,12 +85,14 @@
     table,
     own_table,
     turns,
+    coords,
     grid_u,
     grid_v,
     weighted,
     weights,
     phases,
     phase_u,
+    phase_v,
     kept,
     to_partner,
     from_partner,
@@ -141,7 +140,8 @@
             grid_u[block, HALF * part + 32 * at : HALF * part + 32 * at + 32] = value.astype(jnp.bfloat16)
 
         lanes = pl.ds(block * 128, 128) if isinstance(block, int) else pl.ds(pl.multiple_of(block * 128, 128), 128)
-        chains(baseline[sub, 0:1, lanes], turns, emit)
+        at = 2 * sub
+        chains(coords[at : at + 1, lanes], coords[8 + at : 9 + at, lanes], coords[16 + at : 17 + at, lanes], turns, emit)
 
     def fill_v(sub, block):
         def emit(part, at, value):
@@ -149,16 +149,24 @@
             grid_v[block, first : first + 32] = value.astype(jnp.bfloat16)
 
         lanes = pl.ds(block * 128, 128) if isinstance(block, int) else pl.ds(pl.multiple_of(block * 128, 128), 128)
-        chains(baseline[sub, 1:2, lanes], turns, emit)
-
-    for load in loads[:4]:
-        load.wait()
+        at = 2 * sub + 1
+        chains(coords[at : at + 1, lanes], coords[8 + at : 9 + at, lanes], coords[16 + at : 17 + at, lanes], turns, emit)
+
+    loads[0].wait()
+    for sub in range(OWN):
+        coords[2 * sub : 2 * sub + 2] = baseline[sub]
+    small = coords[0:8] * (1.0 / 32.0)
+    coords[8:16] = cos_turns(small)
+    coords[16:24] = cos_turns(small - 0.25)
 
     def first_fill(block, inner):
         fill_u(0, block)
         return inner
 
     lax.fori_loop(0, 8, first_fill, 0)
+
+    for load in loads[1:]:
+        load.wait()
 
     pixel = STRIDE * lax.broadcasted_iota(jnp.int32, (8, SIDE), 1) - IMAGE // 2
     subgrid = lax.broadcasted_iota(jnp.int32, (8, SIDE), 0)
@@ -172,25 +180,27 @@
         size = jnp.broadcast_to(taper[axis] * factor, (8, SIDE))
         parts.append(size * cos_turns(frac))
         parts.append(size * cos_turns(frac - 0.25))
-    square = jnp.concatenate(parts + [jnp.zeros((ROWS - 32, SIDE), jnp.float32)], axis=0)
+    for part in range(2):
+        chips = parts[part][:, 0:128]
+        for other in range(1, 8):
+            chips = jnp.where(plane == other, parts[part][:, 128 * other : 128 * other + 128], chips)
+        phase_u[part] = chips
+    square = jnp.concatenate(parts[2:4] + [jnp.zeros((ROWS - 16, SIDE), jnp.float32)], axis=0)
     phases[...] = square.T
 
-    for load in loads[4:]:
-        load.wait()
-
-    for near in range(2):
-        place = pl.multiple_of(plane * ROWS + (core if near == 0 else 1 - core) * 64, 64)
-        some = phases[pl.ds(place, 64), :]
-        for sub in range(OWN):
-            for part in range(2):
-                column = some[:, 8 * part + sub : 8 * part + sub + 1]
-                phase_u[sub, near, part] = jnp.broadcast_to(column, (64, 128))
-        cos_rows = table[pl.ds(place, 64), 0:HALF]
-        sin_rows = table[pl.ds(place, 64), HALF:SIDE]
-        own_table[128 * near : 128 * near + 64, 0:HALF] = cos_rows
-        own_table[128 * near : 128 * near + 64, HALF:SIDE] = cos_rows
-        own_table[128 * near + 64 : 128 * near + 128, 0:HALF] = sin_rows
-        own_table[128 * near + 64 : 128 * near + 128, HALF:SIDE] = -sin_rows
+    def spread(number):
+        sub, part, quarter = number // 8, number // 4 % 2, number % 4
+        place = slice(256 * quarter, 256 * quarter + 256)
+        column = phases[place, 8 * part + sub : 8 * part + sub + 1]
+        phase_v[sub, part, place] = jnp.broadcast_to(column, (256, 128))
+
+    place = pl.ds(pl.multiple_of(plane * ROWS, ROWS), ROWS)
+    cos_rows = table[place, 0:HALF]
+    sin_rows = table[place, HALF:SIDE]
+    own_table[0:ROWS, 0:HALF] = cos_rows
+    own_table[0:ROWS, HALF:SIDE] = cos_rows
+    own_table[ROWS : 2 * ROWS, 0:HALF] = sin_rows
+    own_table[ROWS : 2 * ROWS, HALF:SIDE] = -sin_rows
 
     slot = lax.broadcasted_iota(jnp.int32, (2, SIDE), 1)
     for sub in range(OWN):
@@ -203,19 +213,9 @@
         lanes = pl.ds(step * 256, 256)
         vis_re = visibility[sub, 0:1, lanes]
         vis_im = visibility[sub, 1:2, lanes]
-        for near in range(2):
-            real = product[128 * near : 128 * near + 64]
-            imag = product[128 * near + 64 : 128 * near + 128]
-            mid_re = real * vis_re - imag * vis_im
-            mid_im = real * vis_im + imag * vis_re
-            turn_re = jnp.concatenate([phase_u[sub, near, 0]] * 2, axis=1)
-            turn_im = jnp.concatenate([phase_u[sub, near, 1]] * 2, axis=1)
-            out_re = mid_re * turn_re - mid_im * turn_im
-            out_im = mid_re * turn_im + mid_im * turn_re
-            both = jnp.concatenate([out_re, out_im], axis=0).astype(jnp.bfloat16)
-            weighted[near, lanes, :] = both.T
-
-    sign = jnp.where(lax.broadcasted_iota(jnp.int32, (128, 128), 1) < 64, -1.0, 1.0)
+        real, imag = product[0:ROWS], product[ROWS : 2 * ROWS]
+        weighted[0, lanes, :] = (real * vis_re - imag * vis_im).astype(jnp.bfloat16).T
+        weighted[1, lanes, :] = (real * vis_im + imag * vis_re).astype(jnp.bfloat16).T
 
     def columns_of_grid(sub, step):
         place = pl.ds(step * 256, 256)
@@ -225,35 +225,25 @@
         plus, minus = product[0:128], product[128:256]
         at = pl.ds(step * 128, 128)
         at_odd = pl.ds(HALF + step * 128, 128)
-        total = (plus + minus).astype(jnp.bfloat16)
-        diff = plus - minus
-        for near in range(2):
-            lanes = slice(128 * near, 128 * near + 128)
-            weights[sub, near, at, :] = total[:, lanes]
-            weights[sub, near, at_odd, :] = (pltpu.roll(diff[:, lanes], 64, 1) * sign).astype(jnp.bfloat16)
-
-    def one_subgrid(sub, carry):
-        def first_half(step, inner):
+        weights[sub, 0, at, :] = (plus[:, 0:128] + minus[:, 0:128]).astype(jnp.bfloat16)
+        weights[sub, 1, at, :] = (plus[:, 128:256] + minus[:, 128:256]).astype(jnp.bfloat16)
+        weights[sub, 0, at_odd, :] = (minus[:, 128:256] - plus[:, 128:256]).astype(jnp.bfloat16)
+        weights[sub, 1, at_odd, :] = (plus[:, 0:128] - minus[:, 0:128]).astype(jnp.bfloat16)
+
+    for sub in range(OWN):
+        for step in range(4):
             rows_of_image(sub, step)
             fill_v(sub, 2 * step)
             fill_v(sub, 2 * step + 1)
-            return inner
-
-        def second_half(step, inner):
+            spread(8 * sub + step)
+        for step in range(4):
             columns_of_grid(sub, step)
-            fill_u(jnp.minimum(sub + 1, OWN - 1), 2 * step)
-            fill_u(jnp.minimum(sub + 1, OWN - 1), 2 * step + 1)
-            return inner
-
-        for step in range(4):
-            first_half(step, 0)
-        for step in range(4):
-            second_half(step, 0)
-        return carry
-
-    lax.fori_loop(0, OWN, one_subgrid, 0)
-
-    sign_row = jnp.where(lax.broadcasted_iota(jnp.int32, (256, 128), 1) < 64, -1.0, 1.0)
+            spread(8 * sub + 4 + step)
+            if sub + 1 < OWN:
+                fill_u(sub + 1, 2 * step)
+                fill_u(sub + 1, 2 * step + 1)
+
+    low_lanes = lax.broadcasted_iota(jnp.int32, (256, 128), 1) < 64
 
     def pair_copy(step):
         return pltpu.make_async_remote_copy(
@@ -281,18 +271,22 @@
         to_x = lax.rem(here_x + 3 - step, 4)
         place = pl.ds(pl.multiple_of(to_x * 256, 256), 256)
         lhs = table[place, :]
-        columns = phases[place, :]
-        sums = [jnp.zeros((256, 128), jnp.float32)] * 2
+        sum_re = jnp.zeros((256, 128), jnp.float32)
+        sum_im = jnp.zeros((256, 128), jnp.float32)
         for sub in range(OWN):
             rhs = jnp.concatenate([weights[sub, 0], weights[sub, 1]], axis=1)
             product = jnp.dot(lhs, rhs, preferred_element_type=jnp.float32)
-            turn_re = jnp.broadcast_to(columns[:, 16 + sub : 17 + sub], (256, 128))
-            turn_im = jnp.broadcast_to(columns[:, 24 + sub : 25 + sub], (256, 128)) * sign_row
-            for near in range(2):
-                part = product[:, 128 * near : 128 * near + 128]
-                sums[near] = sums[near] + (part * turn_re + pltpu.roll(part, 64, 1) * turn_im)
-        kept[step] = sums[0]
-        to_partner[step] = sums[1].astype(jnp.bfloat16)
+            real, imag = product[:, 0:128], product[:, 128:256]
+            row_re, row_im = phase_u[0, sub : sub + 1], phase_u[1, sub : sub + 1]
+            mid_re = real * row_re - imag * row_im
+            mid_im = real * row_im + imag * row_re
+            turn_re, turn_im = phase_v[sub, 0, place], phase_v[sub, 1, place]
+            sum_re = sum_re + (mid_re * turn_re - mid_im * turn_im)
+            sum_im = sum_im + (mid_re * turn_im + mid_im * turn_re)
+        first = jnp.where(low_lanes, sum_re, pltpu.roll(sum_im, 64, 1))
+        second = jnp.where(low_lanes, pltpu.roll(sum_re, 64, 1), sum_im)
+        kept[step] = jnp.where(core == 0, first, second)
+        to_partner[step] = jnp.where(core == 0, second, first).astype(jnp.bfloat16)
 
     def finish(step):
         pair_copy(step).wait_recv()
@@ -311,8 +305,9 @@
         if step == 0:
             pl.semaphore_wait(barrier, 16)
         pair_copy(step).start()
-        if step > 0:
-            finish(step - 1)
+        if step > 1:
+            finish(step - 2)
+    finish(2)
     finish(3)
 
     total = kept[3, pl.ds(pl.multiple_of(here_y * 64, 64), 64), :]
@@ -349,12 +344,14 @@
             pltpu.VMEM((SIDE, SIDE), half),
             pltpu.VMEM((2 * ROWS, SIDE), half),
             pltpu.VMEM((64, 128), full),
+            pltpu.VMEM((24, SIDE), full),
             pltpu.VMEM((8, SIDE, 128), half),
             pltpu.VMEM((8, SIDE, 128), half),
             pltpu.VMEM((2, SIDE, 128), half),
             pltpu.VMEM((OWN, 2, SIDE, 128), half),
             pltpu.VMEM((SIDE, 128), full),
-            pltpu.VMEM((OWN, 2, 2, 64, 128), full),
+            pltpu.VMEM((2, 8, 128), full),
+            pltpu.VMEM((OWN, 2, SIDE, 128), full),
             pltpu.VMEM((4, 256, 128), full),
             pltpu.VMEM((4, 256, 128), half),
             pltpu.VMEM((4, 256, 128), half),

time: 26.9 us -> 25.8 us (0.959)
  Pallas kernels: 25.2 us -> 24.2 us
    pallas_call x1, Pallas kernels: 25.2 us -> 24.2 us  [per_device(): pl.pallas_call(kernel, out_shape=jax.ShapeDtypeStruct((64, 128), full), i...]
where the time goes in v3:
time: 25.8 us; the launch traced here: 25.7 us
  Pallas kernels  24.2 us (94%)
  local copies, waits for them, and re-layouts  1.49 us (6%)
    pallas_call x1, Pallas kernels, per_device(): pl.pallas_call(kernel, out_shape=jax.ShapeDtypeStruct((64, 128), full), i...  24.2 us
    reshape x1, local copies, waits for them, and re-layouts, per_device(): return total.T.reshape(2, 64, 64)  1.49 us

profile of v3, /device:TPU:1, one launch (start us, length us, event | category | flops | bytes accessed | tf_op | source)
XLA Modules:
  0.0 25.7 jit_solution(18230558930130664646)
XLA Ops:
  0.0 24.2 %facet_rows.1 = f32[64,128]{1,0:T(8,128)} custom-call(f32[8,2,1024]{2,1,0:T(2,128)} %visibility_hbm.1, f32[8,2,1024]{2,1,0:T(2,128)} %baseline_hbm.1, s32[2,8]{1,0:T(2,128)} %bitcast.8, s32[8]{0:T(128)} %counts_hbm.1, f32[1,1024]{1,0:T(1,128)} %bitcast.6, f32[1,1024]{1,0:T(1,128)} %bitcast.7, bf16[1024,1024]{1,0:T(8,128)(2,1)} %constant.2.clone.table_hbm), custom_call_target="tpu_custom_call" | custom-call | tf_op jit(solution)/shard_map/facet_rows/pallas_call | solution.py:333
  24.2 1.5 %copy.9 = f32[128,64]{1,0:T(8,128)} copy(f32[128,64]{0,1:T(8,128)} %bitcast.5) | data formatting | bytes 65536 | tf_op jit(solution)/shard_map/reshape | solution.py:379

commit v4 on v3

--- a/solution.py
+++ b/solution.py
@@ -14,6 +14,7 @@
 HALF = SIDE // 2
 STRIDE = IMAGE // SIDE - 1
 OWN = 4
+ORDER = (2, 3, 1, 0)
 ROWS = 128
 MESH = pl.DeviceIdType.MESH
 
@@ -94,13 +95,9 @@
     phase_u,
     phase_v,
     kept,
-    to_partner,
-    from_partner,
     blocks,
     slots,
     load_sem,
-    pair_send,
-    pair_recv,
     block_send,
     block_recv,
 ):
@@ -129,7 +126,8 @@
     pl.semaphore_signal(barrier, inc=1, device_id={"col": partner, "row": row}, device_id_type=MESH)
     for step in range(1, 16):
         other = lax.rem(row + step, 16)
-        pl.semaphore_signal(barrier, inc=1, device_id={"col": col, "row": other}, device_id_type=MESH)
+        for near in (col, partner):
+            pl.semaphore_signal(barrier, inc=1, device_id={"col": near, "row": other}, device_id_type=MESH)
 
     circle = lax.broadcasted_iota(jnp.int32, (32, 128), 0).astype(jnp.float32) * (1.0 / 32.0)
     turns[0:32] = -2.0 * cos_turns(circle)
@@ -245,30 +243,24 @@
 
     low_lanes = lax.broadcasted_iota(jnp.int32, (256, 128), 1) < 64
 
-    def pair_copy(step):
+    def block_copy(step, hop, side):
+        to_x = lax.rem(here_x + ORDER[step], 4)
+        to_y = lax.rem(here_y + hop, 4)
         return pltpu.make_async_remote_copy(
-            src_ref=to_partner.at[step],
-            dst_ref=from_partner.at[step],
-            send_sem=pair_send.at[step],
-            recv_sem=pair_recv.at[step],
-            device_id={"col": partner, "row": row},
+            src_ref=blocks.at[step, side, pl.ds(pl.multiple_of(to_y * 64, 64), 64)],
+            dst_ref=slots.at[step, hop, side],
+            send_sem=block_send.at[step, hop, side],
+            recv_sem=block_recv.at[step, hop, side],
+            device_id={"col": partner if side else col, "row": to_x * 4 + to_y},
             device_id_type=MESH,
         )
 
-    def block_copy(step, hop):
-        to_x = lax.rem(here_x + 3 - step, 4)
-        to_y = lax.rem(here_y + hop, 4)
-        return pltpu.make_async_remote_copy(
-            src_ref=blocks.at[step, hop],
-            dst_ref=slots.at[step, hop],
-            send_sem=block_send.at[step, hop],
-            recv_sem=block_recv.at[step, hop],
-            device_id={"col": col, "row": to_x * 4 + to_y},
-            device_id_type=MESH,
-        )
+    def copies_of(step):
+        away = [(hop, side) for hop in (2, 1, 3, 0) for side in (0, 1)]
+        return away if step < 3 else away[:6] + [(0, 1)]
 
     def transform(step):
-        to_x = lax.rem(here_x + 3 - step, 4)
+        to_x = lax.rem(here_x + ORDER[step], 4)
         place = pl.ds(pl.multiple_of(to_x * 256, 256), 256)
         lhs = table[place, :]
         sum_re = jnp.zeros((256, 128), jnp.float32)
@@ -285,45 +277,28 @@
             sum_im = sum_im + (mid_re * turn_im + mid_im * turn_re)
         first = jnp.where(low_lanes, sum_re, pltpu.roll(sum_im, 64, 1))
         second = jnp.where(low_lanes, pltpu.roll(sum_re, 64, 1), sum_im)
-        kept[step] = jnp.where(core == 0, first, second)
-        to_partner[step] = jnp.where(core == 0, second, first).astype(jnp.bfloat16)
-
-    def finish(step):
-        pair_copy(step).wait_recv()
-        both = kept[step] + from_partner[step].astype(jnp.float32)
-        kept[step] = both
-        for hop in range(4):
-            to_y = lax.rem(here_y + hop, 4)
-            if step == 3 and hop == 0:
-                continue
-            piece = kept[step, pl.ds(pl.multiple_of(to_y * 64, 64), 64), :]
-            blocks[step, hop] = piece.astype(jnp.bfloat16)
-            block_copy(step, hop).start()
+        mine = jnp.where(core == 0, first, second)
+        if step == 3:
+            kept[...] = mine
+        blocks[step, 0] = mine.astype(jnp.bfloat16)
+        blocks[step, 1] = jnp.where(core == 0, second, first).astype(jnp.bfloat16)
 
     for step in range(4):
         transform(step)
         if step == 0:
-            pl.semaphore_wait(barrier, 16)
-        pair_copy(step).start()
-        if step > 1:
-            finish(step - 2)
-    finish(2)
-    finish(3)
-
-    total = kept[3, pl.ds(pl.multiple_of(here_y * 64, 64), 64), :]
+            pl.semaphore_wait(barrier, 31)
+        for hop, side in copies_of(step):
+            block_copy(step, hop, side).start()
+
+    total = kept[pl.ds(pl.multiple_of(here_y * 64, 64), 64), :]
     for step in range(4):
-        for hop in range(4):
-            if step == 3 and hop == 0:
-                continue
-            block_copy(step, hop).wait_recv()
-            total = total + slots[step, hop].astype(jnp.float32)
+        for hop, side in copies_of(step):
+            block_copy(step, hop, side).wait_recv()
+            total = total + slots[step, hop, side].astype(jnp.float32)
     result[...] = total
     for step in range(4):
-        pair_copy(step).wait_send()
-        for hop in range(4):
-            if step == 3 and hop == 0:
-                continue
-            block_copy(step, hop).wait_send()
+        for hop, side in copies_of(step):
+            block_copy(step, hop, side).wait_send()
 
 
 def per_device(visibility, baseline, offsets, counts, taper_x, taper_y):
@@ -352,29 +327,30 @@
             pltpu.VMEM((SIDE, 128), full),
             pltpu.VMEM((2, 8, 128), full),
             pltpu.VMEM((OWN, 2, SIDE, 128), full),
-            pltpu.VMEM((4, 256, 128), full),
-            pltpu.VMEM((4, 256, 128), half),
-            pltpu.VMEM((4, 256, 128), half),
-            pltpu.VMEM((4, 4, 64, 128), half),
-            pltpu.VMEM((4, 4, 64, 128), half),
+            pltpu.VMEM((256, 128), full),
+            pltpu.VMEM((4, 2, 256, 128), half),
+            pltpu.VMEM((4, 4, 2, 64, 128), half),
             pltpu.SemaphoreType.DMA((7,)),
-            pltpu.SemaphoreType.DMA((4,)),
-            pltpu.SemaphoreType.DMA((4,)),
-            pltpu.SemaphoreType.DMA((4, 4)),
-            pltpu.SemaphoreType.DMA((4, 4)),
+            pltpu.SemaphoreType.DMA((4, 4, 2)),
+            pltpu.SemaphoreType.DMA((4, 4, 2)),
         ],
         compiler_params=pltpu.CompilerParams(
-            collective_id=0, has_side_effects=True, vmem_limit_bytes=67043328
+            collective_id=0, has_side_effects=True, vmem_limit_bytes=48 * 1024 * 1024
         ),
         name="facet_rows",
     )(
-        visibility,
-        baseline,
-        offsets.T,
-        counts,
-        taper_x.reshape(1, SIDE),
-        taper_y.reshape(1, SIDE),
-        jnp.asarray(half_table()),
+        *(
+            pltpu.with_memory_space_constraint(array, pltpu.HBM)
+            for array in (
+                visibility,
+                baseline,
+                offsets.T,
+                counts,
+                taper_x.reshape(1, SIDE),
+                taper_y.reshape(1, SIDE),
+                jnp.asarray(half_table()),
+            )
+        )
     )
     return total.T.reshape(2, 64, 64)
 

time: 25.8 us -> 25.1 us (0.973)
  local copies, waits for them, and re-layouts: 1.49 us -> 0.73 us
    reshape x1, local copies, waits for them, and re-layouts: 1.49 us -> 0.73 us  [per_device(): return total.T.reshape(2, 64, 64)]
where the time goes in v4:
time: 25.1 us; the launch traced here: 25 us
  Pallas kernels  24.2 us (96%)
  local copies, waits for them, and re-layouts  0.73 us (3%)
    pallas_call x1, Pallas kernels, per_device(): pl.pallas_call(kernel, out_shape=jax.ShapeDtypeStruct((64, 128), full), i...  24.2 us
    reshape x1, local copies, waits for them, and re-layouts, per_device(): return total.T.reshape(2, 64, 64)  0.73 us

profile of v4, /device:TPU:1, one launch (start us, length us, event | category | flops | bytes accessed | tf_op | source)
XLA Modules:
  0.0 25.0 jit_solution(17723873608409756083)
XLA Ops:
  0.0 24.2 %facet_rows.1 = f32[64,128]{1,0:T(8,128)S(1)} custom-call(f32[8,2,1024]{2,1,0:T(2,128)} %visibility_hbm.1, f32[8,2,1024]{2,1,0:T(2,128)} %baseline_hbm.1, s32[2,8]{1,0:T(2,128)} %bitcast.8, s32[8]{0:T(128)} %counts_hbm.1, f32[1,1024]{1,0:T(1,128)} %bitcast.6, f32[1,1024]{1,0:T(1,128)} %bitcast.7, bf16[1024,1024]{1,0:T(8,128)(2,1)} %constant.2.clone.table_hbm), custom_call_target="tpu_custom_call" | custom-call | tf_op jit(solution)/shard_map/facet_rows/pallas_call | solution.py:308
  24.2 0.7 %copy.9 = f32[128,64]{1,0:T(8,128)} copy(f32[128,64]{0,1:T(8,128)S(1)} %bitcast.5) | data formatting | bytes 65536 | tf_op jit(solution)/shard_map/reshape | solution.py:355

commit v5 on v4

--- a/solution.py
+++ b/solution.py
@@ -42,7 +42,8 @@
     pixel = STRIDE * np.arange(SIDE, dtype=np.int64) - IMAGE // 2
     odd = 2 * np.arange(HALF, dtype=np.int64) + 1
     angle = (2.0 * np.pi / (2 * IMAGE)) * np.mod(pixel[:, None] * odd[None, :], 2 * IMAGE)
-    return np.concatenate([np.cos(angle), np.sin(angle)], axis=1).astype(jnp.bfloat16)
+    both = np.stack([np.cos(angle).reshape(SIDE, 4, 128), np.sin(angle).reshape(SIDE, 4, 128)], axis=2)
+    return both.reshape(SIDE, SIDE).astype(jnp.bfloat16)
 
 
 def chains(coord, cos_here, sin_here, turns, emit):
@@ -91,13 +92,17 @@
     grid_v,
     weighted,
     weights,
-    phases,
-    phase_u,
-    phase_v,
+    outgoing,
+    incoming,
+    advance,
+    window,
+    sums,
     kept,
     blocks,
     slots,
     load_sem,
+    pair_send,
+    pair_recv,
     block_send,
     block_recv,
 ):
@@ -126,12 +131,15 @@
     pl.semaphore_signal(barrier, inc=1, device_id={"col": partner, "row": row}, device_id_type=MESH)
     for step in range(1, 16):
         other = lax.rem(row + step, 16)
-        for near in (col, partner):
-            pl.semaphore_signal(barrier, inc=1, device_id={"col": near, "row": other}, device_id_type=MESH)
+        pl.semaphore_signal(barrier, inc=1, device_id={"col": col, "row": other}, device_id_type=MESH)
 
     circle = lax.broadcasted_iota(jnp.int32, (32, 128), 0).astype(jnp.float32) * (1.0 / 32.0)
     turns[0:32] = -2.0 * cos_turns(circle)
     turns[32:64] = -2.0 * cos_turns(circle - 0.25)
+
+    def shift_of(axis, sub):
+        which = core * OWN + sub if sub < OWN else (1 - core) * OWN + sub - OWN
+        return 2 * offsets[axis, which] + (SIDE - 1)
 
     def fill_u(sub, block):
         def emit(part, at, value):
@@ -166,39 +174,35 @@
     for load in loads[1:]:
         load.wait()
 
-    pixel = STRIDE * lax.broadcasted_iota(jnp.int32, (8, SIDE), 1) - IMAGE // 2
-    subgrid = lax.broadcasted_iota(jnp.int32, (8, SIDE), 0)
+    which_row = lax.broadcasted_iota(jnp.int32, (8, 128), 0)
+    shift = jnp.zeros((8, 128), jnp.int32)
+    for sub in range(2 * OWN):
+        shift = jnp.where(which_row == sub, shift_of(1, sub), shift)
+    angle = (8 * STRIDE * shift) & (2 * IMAGE - 1)
+    advance[...] = 2.0 * cos_turns(angle.astype(jnp.float32) * (1.0 / (2 * IMAGE)))
+
+    chips = taper[0][:, 0:128]
+    for other in range(1, 8):
+        chips = jnp.where(plane == other, taper[0][:, 128 * other : 128 * other + 128], chips)
+    chips = jnp.broadcast_to(chips, (8, 128))
+    turned = pltpu.roll(chips, 64, 1)
+    low = lax.broadcasted_iota(jnp.int32, (8, 128), 1) < 64
     scale = 4.0 / (SIDE * math.sqrt(float(128 * SIDE)))
-    parts = []
-    for axis, factor in ((0, 1.0), (1, scale)):
-        shift = jnp.zeros((8, SIDE), jnp.int32)
-        for sub in range(OWN):
-            shift = jnp.where(subgrid == sub, 2 * offsets[axis, core * OWN + sub] + (SIDE - 1), shift)
-        frac = ((pixel * shift) & (2 * IMAGE - 1)).astype(jnp.float32) * (1.0 / (2 * IMAGE))
-        size = jnp.broadcast_to(taper[axis] * factor, (8, SIDE))
-        parts.append(size * cos_turns(frac))
-        parts.append(size * cos_turns(frac - 0.25))
-    for part in range(2):
-        chips = parts[part][:, 0:128]
-        for other in range(1, 8):
-            chips = jnp.where(plane == other, parts[part][:, 128 * other : 128 * other + 128], chips)
-        phase_u[part] = chips
-    square = jnp.concatenate(parts[2:4] + [jnp.zeros((ROWS - 16, SIDE), jnp.float32)], axis=0)
-    phases[...] = square.T
-
-    def spread(number):
-        sub, part, quarter = number // 8, number // 4 % 2, number % 4
-        place = slice(256 * quarter, 256 * quarter + 256)
-        column = phases[place, 8 * part + sub : 8 * part + sub + 1]
-        phase_v[sub, part, place] = jnp.broadcast_to(column, (256, 128))
-
-    place = pl.ds(pl.multiple_of(plane * ROWS, ROWS), ROWS)
-    cos_rows = table[place, 0:HALF]
-    sin_rows = table[place, HALF:SIDE]
-    own_table[0:ROWS, 0:HALF] = cos_rows
-    own_table[0:ROWS, HALF:SIDE] = cos_rows
-    own_table[ROWS : 2 * ROWS, 0:HALF] = sin_rows
-    own_table[ROWS : 2 * ROWS, HALF:SIDE] = -sin_rows
+    along_i = jnp.where(core == 0, jnp.where(low, chips, turned), jnp.where(low, turned, chips)) * scale
+    columns = taper[1][:, 0:128]
+    for other in range(1, 8):
+        columns = jnp.where(row // 2 == other, taper[1][:, 128 * other : 128 * other + 128], columns)
+    window[...] = jnp.broadcast_to(columns, (128, 128)).T * along_i[0:1]
+
+    for near in range(2):
+        place = pl.ds(pl.multiple_of(plane * ROWS + (core if near == 0 else 1 - core) * 64, 64), 64)
+        for tile in range(4):
+            cos_rows = table[place, 256 * tile : 256 * tile + 128]
+            sin_rows = table[place, 256 * tile + 128 : 256 * tile + 256]
+            for half, sin_half in ((0, sin_rows), (HALF, -sin_rows)):
+                lanes = slice(half + 128 * tile, half + 128 * tile + 128)
+                own_table[128 * near : 128 * near + 64, lanes] = cos_rows
+                own_table[128 * near + 64 : 128 * near + 128, lanes] = sin_half
 
     slot = lax.broadcasted_iota(jnp.int32, (2, SIDE), 1)
     for sub in range(OWN):
@@ -211,9 +215,14 @@
         lanes = pl.ds(step * 256, 256)
         vis_re = visibility[sub, 0:1, lanes]
         vis_im = visibility[sub, 1:2, lanes]
-        real, imag = product[0:ROWS], product[ROWS : 2 * ROWS]
-        weighted[0, lanes, :] = (real * vis_re - imag * vis_im).astype(jnp.bfloat16).T
-        weighted[1, lanes, :] = (real * vis_im + imag * vis_re).astype(jnp.bfloat16).T
+        for near in range(2):
+            real = product[128 * near : 128 * near + 64]
+            imag = product[128 * near + 64 : 128 * near + 128]
+            out_re = real * vis_re - imag * vis_im
+            out_im = real * vis_im + imag * vis_re
+            weighted[near, lanes, :] = jnp.concatenate([out_re, out_im], axis=0).astype(jnp.bfloat16).T
+
+    sign = jnp.where(lax.broadcasted_iota(jnp.int32, (128, 128), 1) < 64, -1.0, 1.0)
 
     def columns_of_grid(sub, step):
         place = pl.ds(step * 256, 256)
@@ -221,84 +230,123 @@
         rhs = jnp.concatenate([weighted[0], weighted[1]], axis=1)
         product = jnp.dot(lhs, rhs, preferred_element_type=jnp.float32)
         plus, minus = product[0:128], product[128:256]
-        at = pl.ds(step * 128, 128)
-        at_odd = pl.ds(HALF + step * 128, 128)
-        weights[sub, 0, at, :] = (plus[:, 0:128] + minus[:, 0:128]).astype(jnp.bfloat16)
-        weights[sub, 1, at, :] = (plus[:, 128:256] + minus[:, 128:256]).astype(jnp.bfloat16)
-        weights[sub, 0, at_odd, :] = (minus[:, 128:256] - plus[:, 128:256]).astype(jnp.bfloat16)
-        weights[sub, 1, at_odd, :] = (plus[:, 0:128] - minus[:, 0:128]).astype(jnp.bfloat16)
+        for near, target in ((0, weights), (1, outgoing)):
+            lanes = slice(128 * near, 128 * near + 128)
+            diff = pltpu.roll(plus[:, lanes] - minus[:, lanes], 64, 1) * sign
+            target[sub, 256 * step : 256 * step + 128] = (plus[:, lanes] + minus[:, lanes]).astype(jnp.bfloat16)
+            target[sub, 256 * step + 128 : 256 * step + 256] = diff.astype(jnp.bfloat16)
+
+    def pair_copy(number):
+        some = (pl.ds(0, 2), pl.ds(2, 1), pl.ds(3, 1))[number]
+        return pltpu.make_async_remote_copy(
+            src_ref=outgoing.at[some],
+            dst_ref=incoming.at[some],
+            send_sem=pair_send.at[number],
+            recv_sem=pair_recv.at[number],
+            device_id={"col": partner, "row": row},
+            device_id_type=MESH,
+        )
 
     for sub in range(OWN):
         for step in range(4):
             rows_of_image(sub, step)
             fill_v(sub, 2 * step)
             fill_v(sub, 2 * step + 1)
-            spread(8 * sub + step)
+            if sub > 1 and step == 1:
+                if sub == 2:
+                    pl.semaphore_wait(barrier, 16)
+                pair_copy(sub - 2).start()
         for step in range(4):
             columns_of_grid(sub, step)
-            spread(8 * sub + 4 + step)
             if sub + 1 < OWN:
                 fill_u(sub + 1, 2 * step)
                 fill_u(sub + 1, 2 * step + 1)
-
-    low_lanes = lax.broadcasted_iota(jnp.int32, (256, 128), 1) < 64
-
-    def block_copy(step, hop, side):
+    pair_copy(2).start()
+
+
+    def block_copy(step, hop):
         to_x = lax.rem(here_x + ORDER[step], 4)
         to_y = lax.rem(here_y + hop, 4)
         return pltpu.make_async_remote_copy(
-            src_ref=blocks.at[step, side, pl.ds(pl.multiple_of(to_y * 64, 64), 64)],
-            dst_ref=slots.at[step, hop, side],
-            send_sem=block_send.at[step, hop, side],
-            recv_sem=block_recv.at[step, hop, side],
-            device_id={"col": partner if side else col, "row": to_x * 4 + to_y},
+            src_ref=blocks.at[step, pl.ds(pl.multiple_of(to_y * 64, 64), 64)],
+            dst_ref=slots.at[step, hop],
+            send_sem=block_send.at[step, hop],
+            recv_sem=block_recv.at[step, hop],
+            device_id={"col": col, "row": to_x * 4 + to_y},
             device_id_type=MESH,
         )
 
-    def copies_of(step):
-        away = [(hop, side) for hop in (2, 1, 3, 0) for side in (0, 1)]
-        return away if step < 3 else away[:6] + [(0, 1)]
-
-    def transform(step):
+    def hops_of(step):
+        return (2, 1, 3, 0) if step < 3 else (2, 1, 3)
+
+    lane = lax.broadcasted_iota(jnp.int32, (8, 128), 1)
+    sample = STRIDE * (plane * ROWS + core * 64 + (lane & 63)) - IMAGE // 2
+    cross_sign = jnp.where(lane < 64, 1.0, -1.0)
+
+    def transform(step, subs):
         to_x = lax.rem(here_x + ORDER[step], 4)
         place = pl.ds(pl.multiple_of(to_x * 256, 256), 256)
         lhs = table[place, :]
-        sum_re = jnp.zeros((256, 128), jnp.float32)
-        sum_im = jnp.zeros((256, 128), jnp.float32)
-        for sub in range(OWN):
-            rhs = jnp.concatenate([weights[sub, 0], weights[sub, 1]], axis=1)
+        straight, crossed = [None] * 32, [None] * 32
+        if subs[0] > 0:
+            straight = [sums[step, 0, 8 * i : 8 * i + 8] for i in range(32)]
+            crossed = [sums[step, 1, 8 * i : 8 * i + 8] for i in range(32)]
+        for sub in subs:
+            rhs = jnp.concatenate([weights[sub], incoming[sub]], axis=1)
             product = jnp.dot(lhs, rhs, preferred_element_type=jnp.float32)
-            real, imag = product[:, 0:128], product[:, 128:256]
-            row_re, row_im = phase_u[0, sub : sub + 1], phase_u[1, sub : sub + 1]
-            mid_re = real * row_re - imag * row_im
-            mid_im = real * row_im + imag * row_re
-            turn_re, turn_im = phase_v[sub, 0, place], phase_v[sub, 1, place]
-            sum_re = sum_re + (mid_re * turn_re - mid_im * turn_im)
-            sum_im = sum_im + (mid_re * turn_im + mid_im * turn_re)
-        first = jnp.where(low_lanes, sum_re, pltpu.roll(sum_im, 64, 1))
-        second = jnp.where(low_lanes, pltpu.roll(sum_re, 64, 1), sum_im)
-        mine = jnp.where(core == 0, first, second)
+            for side in range(2):
+                which = OWN * side + sub
+                shift_u, shift_v = shift_of(0, which), shift_of(1, which)
+                double = advance[which : which + 1]
+
+                def anchor(at):
+                    pixel = STRIDE * (to_x * 256 + 8 * at + which_row) - IMAGE // 2
+                    turns = (pixel * shift_v + sample * shift_u) & (2 * IMAGE - 1)
+                    frac = turns.astype(jnp.float32) * (1.0 / (2 * IMAGE))
+                    return cos_turns(frac), cos_turns(frac - 0.25) * cross_sign
+
+                below, above = anchor(15), anchor(16)
+                for before, now, order in ((below, above, range(16, 32)), (above, below, range(15, -1, -1))):
+                    for at in order:
+                        part = product[8 * at : 8 * at + 8, 128 * side : 128 * side + 128]
+                        add, cross = part * now[0], part * now[1]
+                        straight[at] = add if straight[at] is None else straight[at] + add
+                        crossed[at] = cross if crossed[at] is None else crossed[at] + cross
+                        after = tuple(double * b - a for a, b in zip(before, now))
+                        before, now = now, after
+        if subs[-1] < OWN - 1:
+            sums[step, 0] = jnp.concatenate(straight, axis=0)
+            sums[step, 1] = jnp.concatenate(crossed, axis=0)
+            return
+        total = jnp.concatenate(straight, axis=0) + pltpu.roll(jnp.concatenate(crossed, axis=0), 64, 1)
         if step == 3:
-            kept[...] = mine
-        blocks[step, 0] = mine.astype(jnp.bfloat16)
-        blocks[step, 1] = jnp.where(core == 0, second, first).astype(jnp.bfloat16)
-
+            kept[...] = total
+        blocks[step] = total.astype(jnp.bfloat16)
+
+    early, late = (0, 1, 2), (3,)
+    pair_copy(0).wait_recv()
+    pair_copy(1).wait_recv()
     for step in range(4):
-        transform(step)
-        if step == 0:
-            pl.semaphore_wait(barrier, 31)
-        for hop, side in copies_of(step):
-            block_copy(step, hop, side).start()
+        transform(step, early)
+    pair_copy(2).wait_recv()
+    for steps in ((0, 1), (2, 3)):
+        for step in steps:
+            transform(step, late)
+        for step in steps:
+            for hop in hops_of(step):
+                block_copy(step, hop).start()
 
     total = kept[pl.ds(pl.multiple_of(here_y * 64, 64), 64), :]
     for step in range(4):
-        for hop, side in copies_of(step):
-            block_copy(step, hop, side).wait_recv()
-            total = total + slots[step, hop, side].astype(jnp.float32)
-    result[...] = total
+        for hop in hops_of(step):
+            block_copy(step, hop).wait_recv()
+            total = total + slots[step, hop].astype(jnp.float32)
+    result[...] = total * window[pl.ds(pl.multiple_of(lax.rem(row, 2) * 64, 64), 64), :]
+    for number in range(3):
+        pair_copy(number).wait_send()
     for step in range(4):
-        for hop, side in copies_of(step):
-            block_copy(step, hop, side).wait_send()
+        for hop in hops_of(step):
+            block_copy(step, hop).wait_send()
 
 
 def per_device(visibility, baseline, offsets, counts, taper_x, taper_y):
@@ -323,16 +371,20 @@
             pltpu.VMEM((8, SIDE, 128), half),
             pltpu.VMEM((8, SIDE, 128), half),
             pltpu.VMEM((2, SIDE, 128), half),
-            pltpu.VMEM((OWN, 2, SIDE, 128), half),
-            pltpu.VMEM((SIDE, 128), full),
-            pltpu.VMEM((2, 8, 128), full),
-            pltpu.VMEM((OWN, 2, SIDE, 128), full),
+            pltpu.VMEM((OWN, SIDE, 128), half),
+            pltpu.VMEM((OWN, SIDE, 128), half),
+            pltpu.VMEM((OWN, SIDE, 128), half),
+            pltpu.VMEM((8, 128), full),
+            pltpu.VMEM((128, 128), full),
+            pltpu.VMEM((4, 2, 256, 128), full),
             pltpu.VMEM((256, 128), full),
-            pltpu.VMEM((4, 2, 256, 128), half),
-            pltpu.VMEM((4, 4, 2, 64, 128), half),
+            pltpu.VMEM((4, 256, 128), half),
+            pltpu.VMEM((4, 4, 64, 128), half),
             pltpu.SemaphoreType.DMA((7,)),
-            pltpu.SemaphoreType.DMA((4, 4, 2)),
-            pltpu.SemaphoreType.DMA((4, 4, 2)),
+            pltpu.SemaphoreType.DMA((3,)),
+            pltpu.SemaphoreType.DMA((3,)),
+            pltpu.SemaphoreType.DMA((4, 4)),
+            pltpu.SemaphoreType.DMA((4, 4)),
         ],
         compiler_params=pltpu.CompilerParams(
             collective_id=0, has_side_effects=True, vmem_limit_bytes=48 * 1024 * 1024

time: 25.1 us -> 23.4 us (0.932)
  Pallas kernels: 24.2 us -> 22.6 us
    pallas_call x1, Pallas kernels: 24.2 us -> 22.6 us  [per_device(): pl.pallas_call(kernel, out_shape=jax.ShapeDtypeStruct((64, 128), full), i...]
where the time goes in v5:
time: 23.4 us; the launch traced here: 23.3 us
  Pallas kernels  22.6 us (97%)
  local copies, waits for them, and re-layouts  0.73 us (3%)
    pallas_call x1, Pallas kernels, per_device(): pl.pallas_call(kernel, out_shape=jax.ShapeDtypeStruct((64, 128), full), i...  22.6 us
    reshape x1, local copies, waits for them, and re-layouts, per_device(): return total.T.reshape(2, 64, 64)  0.73 us

profile of v5, /device:TPU:1, one launch (start us, length us, event | category | flops | bytes accessed | tf_op | source)
XLA Modules:
  0.0 23.3 jit_solution(8908675500844924106)
XLA Ops:
  0.0 22.6 %facet_rows.1 = f32[64,128]{1,0:T(8,128)S(1)} custom-call(f32[8,2,1024]{2,1,0:T(2,128)} %visibility_hbm.1, f32[8,2,1024]{2,1,0:T(2,128)} %baseline_hbm.1, s32[2,8]{1,0:T(2,128)} %bitcast.8, s32[8]{0:T(128)} %counts_hbm.1, f32[1,1024]{1,0:T(1,128)} %bitcast.6, f32[1,1024]{1,0:T(1,128)} %bitcast.7, bf16[1024,1024]{1,0:T(8,128)(2,1)} %constant.2.clone.table_hbm), custom_call_target="tpu_custom_call" | custom-call | tf_op jit(solution)/shard_map/facet_rows/pallas_call | solution.py:356
  22.6 0.7 %copy.9 = f32[128,64]{1,0:T(8,128)} copy(f32[128,64]{0,1:T(8,128)S(1)} %bitcast.5) | data formatting | bytes 65536 | tf_op jit(solution)/shard_map/reshape | solution.py:407

commit v6 on v5

--- a/solution.py
+++ b/solution.py
@@ -46,14 +46,24 @@
     return both.reshape(SIDE, SIDE).astype(jnp.bfloat16)
 
 
-def chains(coord, cos_here, sin_here, turns, emit):
-    row = lax.broadcasted_iota(jnp.int32, (32, 128), 0).astype(jnp.float32)
-    near = row - jnp.broadcast_to(coord, (32, 128))
-    multiplier = turns[0:32] * cos_here + turns[32:64] * sin_here
-
-    def anchor(block):
-        dist = near + float(32 * block)
-        return cos_turns(dist * dist * (1.0 / (2 * SIDE)))
+def chains(rows, turns, emit):
+    coord, cos_32, sin_32, cos_128, sin_128 = rows
+    multiplier = turns[0:32] * cos_32 + turns[32:64] * sin_32
+    crossing = turns[32:64] * cos_32 - turns[0:32] * sin_32
+
+    dist = (lax.broadcasted_iota(jnp.int32, (8, 128), 0).astype(jnp.float32) + 480.0) - coord
+    turn = dist * dist * (1.0 / (2 * SIDE))
+    cos_now, sin_now = cos_turns(turn), cos_turns(turn - 0.25)
+    cosines, sines = [cos_now], [sin_now]
+    for step in range(3):
+        cos_at, sin_at = turns[64 + 16 * step : 72 + 16 * step], turns[72 + 16 * step : 80 + 16 * step]
+        cos_step = cos_at * cos_128 + sin_at * sin_128
+        sin_step = sin_at * cos_128 - cos_at * sin_128
+        cos_now, sin_now = cos_now * cos_step - sin_now * sin_step, sin_now * cos_step + cos_now * sin_step
+        cosines.append(cos_now)
+        sines.append(sin_now)
+    below = jnp.concatenate(cosines, axis=0)
+    above = 0.5 * (below * multiplier - jnp.concatenate(sines, axis=0) * crossing)
 
     flip = 7 - lax.broadcasted_iota(jnp.int32, (8, 128), 0)
 
@@ -61,7 +71,6 @@
         pieces = [block[8 * i : 8 * i + 8] for i in range(3, -1, -1)]
         return jnp.concatenate([jnp.take_along_axis(p, flip, axis=0) for p in pieces], axis=0)
 
-    below, above = anchor(15), anchor(16)
     starts = ((multiplier, below, above), tuple(map(reverse, (multiplier, above, below))))
     for part, (factor, before, now) in enumerate(starts):
         for block in range(16):
@@ -136,6 +145,10 @@
     circle = lax.broadcasted_iota(jnp.int32, (32, 128), 0).astype(jnp.float32) * (1.0 / 32.0)
     turns[0:32] = -2.0 * cos_turns(circle)
     turns[32:64] = -2.0 * cos_turns(circle - 0.25)
+    eighth = (lax.broadcasted_iota(jnp.int32, (8, 128), 0).astype(jnp.float32) + 484.0) * (1.0 / 128.0)
+    for step in range(3):
+        turns[64 + 16 * step : 72 + 16 * step] = cos_turns(eighth + step / 16.0)
+        turns[72 + 16 * step : 80 + 16 * step] = cos_turns(eighth + (step / 16.0 - 0.25))
 
     def shift_of(axis, sub):
         which = core * OWN + sub if sub < OWN else (1 - core) * OWN + sub - OWN
@@ -147,7 +160,7 @@
 
         lanes = pl.ds(block * 128, 128) if isinstance(block, int) else pl.ds(pl.multiple_of(block * 128, 128), 128)
         at = 2 * sub
-        chains(coords[at : at + 1, lanes], coords[8 + at : 9 + at, lanes], coords[16 + at : 17 + at, lanes], turns, emit)
+        chains([coords[8 * i + at : 8 * i + at + 1, lanes] for i in range(5)], turns, emit)
 
     def fill_v(sub, block):
         def emit(part, at, value):
@@ -156,7 +169,7 @@
 
         lanes = pl.ds(block * 128, 128) if isinstance(block, int) else pl.ds(pl.multiple_of(block * 128, 128), 128)
         at = 2 * sub + 1
-        chains(coords[at : at + 1, lanes], coords[8 + at : 9 + at, lanes], coords[16 + at : 17 + at, lanes], turns, emit)
+        chains([coords[8 * i + at : 8 * i + at + 1, lanes] for i in range(5)], turns, emit)
 
     loads[0].wait()
     for sub in range(OWN):
@@ -164,6 +177,9 @@
     small = coords[0:8] * (1.0 / 32.0)
     coords[8:16] = cos_turns(small)
     coords[16:24] = cos_turns(small - 0.25)
+    small = coords[0:8] * (1.0 / 128.0)
+    coords[24:32] = cos_turns(small)
+    coords[32:40] = cos_turns(small - 0.25)
 
     def first_fill(block, inner):
         fill_u(0, block)
@@ -340,6 +356,8 @@
     for step in range(4):
         for hop in hops_of(step):
             block_copy(step, hop).wait_recv()
+    for step in range(4):
+        for hop in hops_of(step):
             total = total + slots[step, hop].astype(jnp.float32)
     result[...] = total * window[pl.ds(pl.multiple_of(lax.rem(row, 2) * 64, 64), 64), :]
     for number in range(3):
@@ -366,8 +384,8 @@
             pltpu.VMEM((2, 1, SIDE), full),
             pltpu.VMEM((SIDE, SIDE), half),
             pltpu.VMEM((2 * ROWS, SIDE), half),
-            pltpu.VMEM((64, 128), full),
-            pltpu.VMEM((24, SIDE), full),
+            pltpu.VMEM((112, 128), full),
+            pltpu.VMEM((40, SIDE), full),
             pltpu.VMEM((8, SIDE, 128), half),
             pltpu.VMEM((8, SIDE, 128), half),
             pltpu.VMEM((2, SIDE, 128), half),

time: 23.4 us -> 23.2 us (level)
  Pallas kernels: 22.6 us -> 22.3 us
    pallas_call x1, Pallas kernels: 22.6 us -> 22.3 us  [per_device(): pl.pallas_call(kernel, out_shape=jax.ShapeDtypeStruct((64, 128), full), i...]
where the time goes in v6:
time: 23.2 us; the launch traced here: 23.1 us
  Pallas kernels  22.3 us (96%)
  local copies, waits for them, and re-layouts  0.73 us (3%)
    pallas_call x1, Pallas kernels, per_device(): pl.pallas_call(kernel, out_shape=jax.ShapeDtypeStruct((64, 128), full), i...  22.3 us
    reshape x1, local copies, waits for them, and re-layouts, per_device(): return total.T.reshape(2, 64, 64)  0.73 us

profile of v6, /device:TPU:1, one launch (start us, length us, event | category | flops | bytes accessed | tf_op | source)
XLA Modules:
  0.0 23.1 jit_solution(15433882437663310241)
XLA Ops:
  0.0 22.3 %facet_rows.1 = f32[64,128]{1,0:T(8,128)S(1)} custom-call(f32[8,2,1024]{2,1,0:T(2,128)} %visibility_hbm.1, f32[8,2,1024]{2,1,0:T(2,128)} %baseline_hbm.1, s32[2,8]{1,0:T(2,128)} %bitcast.8, s32[8]{0:T(128)} %counts_hbm.1, f32[1,1024]{1,0:T(1,128)} %bitcast.6, f32[1,1024]{1,0:T(1,128)} %bitcast.7, bf16[1024,1024]{1,0:T(8,128)(2,1)} %constant.2.clone.table_hbm), custom_call_target="tpu_custom_call" | custom-call | tf_op jit(solution)/shard_map/facet_rows/pallas_call | solution.py:374
  22.3 0.7 %copy.9 = f32[128,64]{1,0:T(8,128)} copy(f32[128,64]{0,1:T(8,128)S(1)} %bitcast.5) | data formatting | bytes 65536 | tf_op jit(solution)/shard_map/reshape | solution.py:425

commit v7 on v6

--- a/solution.py
+++ b/solution.py
@@ -345,7 +345,7 @@
     for step in range(4):
         transform(step, early)
     pair_copy(2).wait_recv()
-    for steps in ((0, 1), (2, 3)):
+    for steps in ((0,), (1,), (2,), (3,)):
         for step in steps:
             transform(step, late)
         for step in steps:

time: 23.2 us -> 23.1 us (level)
  no operation moved by 1% of the time
where the time goes in v7:
time: 23.1 us; the launch traced here: 23 us
  Pallas kernels  22.3 us (97%)
  local copies, waits for them, and re-layouts  0.73 us (3%)
    pallas_call x1, Pallas kernels, per_device(): pl.pallas_call(kernel, out_shape=jax.ShapeDtypeStruct((64, 128), full), i...  22.3 us
    reshape x1, local copies, waits for them, and re-layouts, per_device(): return total.T.reshape(2, 64, 64)  0.73 us

profile of v7, /device:TPU:1, one launch (start us, length us, event | category | flops | bytes accessed | tf_op | source)
XLA Modules:
  0.0 23.0 jit_solution(10047475206315613540)
XLA Ops:
  0.0 22.3 %facet_rows.1 = f32[64,128]{1,0:T(8,128)S(1)} custom-call(f32[8,2,1024]{2,1,0:T(2,128)} %visibility_hbm.1, f32[8,2,1024]{2,1,0:T(2,128)} %baseline_hbm.1, s32[2,8]{1,0:T(2,128)} %bitcast.8, s32[8]{0:T(128)} %counts_hbm.1, f32[1,1024]{1,0:T(1,128)} %bitcast.6, f32[1,1024]{1,0:T(1,128)} %bitcast.7, bf16[1024,1024]{1,0:T(8,128)(2,1)} %constant.2.clone.table_hbm), custom_call_target="tpu_custom_call" | custom-call | tf_op jit(solution)/shard_map/facet_rows/pallas_call | solution.py:374
  22.3 0.7 %copy.9 = f32[128,64]{1,0:T(8,128)} copy(f32[128,64]{0,1:T(8,128)S(1)} %bitcast.5) | data formatting | bytes 65536 | tf_op jit(solution)/shard_map/reshape | solution.py:425
